TPU v7x, 128 devices: a whole 4x4x4 slice. The times are simulated.
128 devices in a mesh: ctx: 32 (over x_hi, z, y), tp: 4 (over x_lo, core).
Axes of the slice: x: 4 (x_hi: 2, x_lo: 2; x = x_hi * 2 + x_lo), y: 4, z: 4, core: 2. Of those that a mesh axis runs over, the one named last changes fastest.
Arguments:
- qkv: bfloat16 [3, 8192, 4096], P(None, 'ctx', 'tp'), may hold values from -6 to 6
- filters: bfloat16 [256, 128], P('tp'), may hold values from -0.5 to 0.5
- w_out: bfloat16 [4096, 4096], P(None, 'tp'), may hold values from -0.09375 to 0.09375
- cotangent: bfloat16 [8192, 4096], P(('ctx', 'tp')), may hold values from -24 to 24
- doc_lens: int32 [64], replicated, may hold values from 1 to 384, 8192 in all
Outputs:
- grad_qkv: bfloat16 [3, 8192, 4096], P(None, 'ctx', 'tp')
- grad_filters: float32 [256, 128], P('tp')
- grad_w_out: float32 [4096, 4096], P('ctx', 'tp')
All inputs are finite; a program needn't handle non-finite values.
Results may differ from a plain program's by a relative error of at most 0.005.
Values may be sent and summed in bfloat16 or wider, within the bound.
A program may use at most 128 MiB of HBM per device.

v0:
```python
import math

import jax
import jax.numpy as jnp
from jax import lax
from jax.sharding import PartitionSpec as P


def extended_2(cells, sides, width):
    for axis, dim in sides:
        count = lax.axis_size(axis)
        ends = count - 1
        head = lax.slice_in_dim(cells, 0, width, axis=dim)
        tail = lax.slice_in_dim(cells, cells.shape[dim] - width, cells.shape[dim], axis=dim)
        cells = jnp.concatenate(
            [
                lax.ppermute(tail, axis, [(i, (i + 1) % count) for i in range(ends)]),
                cells,
                lax.ppermute(head, axis, [((i + 1) % count, i) for i in range(ends)]),
            ],
            axis=dim,
        )
    return cells


def banded(filters):
    groups, tap_count = filters.shape
    width = 2 * tap_count
    blank = jnp.zeros((groups, 1), filters.dtype)
    tailing = jnp.zeros((groups, width - tap_count), filters.dtype)
    pattern = jnp.concatenate([blank, jnp.flip(filters, axis=1), tailing], axis=1)
    tiled = jnp.broadcast_to(pattern[:, None, :], (groups, tap_count, width + 1)).reshape(
        groups, tap_count * (width + 1)
    )
    return tiled[:, : tap_count * width].reshape(groups, tap_count, width)


def diagonals(products):
    groups, tap_count, width = products.shape
    flattened = jnp.pad(products.reshape(groups, tap_count * width), ((0, 0), (0, tap_count)))
    sheared = flattened.reshape(groups, tap_count, width + 1)[:, :, 1 : tap_count + 1]
    return jnp.flip(jnp.sum(sheared, axis=1), axis=1)


def doc_reach(positions, doc_lens):
    starts = jnp.cumsum(doc_lens) - doc_lens
    below = jnp.where(starts[None, :] <= positions[:, None], starts[None, :], 0)
    return positions - jnp.max(below, axis=1)


def band_mask(doc_offset, tap_count):
    row_ids = lax.broadcasted_iota(jnp.int32, (tap_count, 2 * tap_count), 0)
    col_ids = lax.broadcasted_iota(jnp.int32, (tap_count, 2 * tap_count), 1)
    return (row_ids - col_ids + tap_count <= doc_offset[:, None]).astype(jnp.float32)


def spread_back(kernel, rows_grad, groups_local, group_width):
    tap_count = rows_grad.shape[0]
    grad_f = rows_grad.astype(jnp.float32).reshape(tap_count, groups_local, group_width)
    spread = jnp.einsum("gij,igc->jgc", kernel, grad_f, precision=lax.Precision.HIGHEST)
    return spread.reshape(2 * tap_count, groups_local * group_width)


def local(qkv, filters, w_out, cotangent, doc_lens):
    queries, key_in, values = (qkv[0], qkv[1], qkv[2])
    tok_ctx, width_local = queries.shape
    span_rows = tok_ctx // 2
    groups_local, tap_count = filters.shape
    group_width = width_local // groups_local
    blocks = span_rows // tap_count
    n_ctx = lax.axis_size("ctx")
    ctx_rank = lax.axis_index("ctx")
    tokens = tok_ctx * n_ctx
    last_rank = ctx_rank == n_ctx - 1
    exact = lax.Precision.HIGHEST
    offsets = jnp.arange(span_rows, dtype=jnp.int32)
    first_pos = ctx_rank * span_rows + offsets
    second_pos = (2 * n_ctx - 1 - ctx_rank) * span_rows + offsets
    doc_offset = jnp.stack([doc_reach(first_pos, doc_lens), doc_reach(second_pos, doc_lens)])
    hidden = (key_in.astype(jnp.float32) * values.astype(jnp.float32)).astype(jnp.bfloat16)
    hidden = hidden.reshape(2, span_rows, width_local)
    outgoing = jnp.concatenate([hidden[1], hidden[0]], axis=0)
    padded = extended_2(outgoing, (("ctx", 0),), tap_count)
    tail_first = padded[:tap_count]
    tail_second = jnp.where(last_rank, hidden[0], padded[3 * tap_count :])
    extended = jnp.concatenate([jnp.stack([tail_first, tail_second]), hidden], axis=1)
    full_cot = lax.all_gather(cotangent, "tp", axis=0, tiled=True)
    grad_y = jnp.dot(full_cot, w_out, preferred_element_type=jnp.float32)
    grad_c = (
        (queries.astype(jnp.float32) * grad_y)
        .astype(jnp.bfloat16)
        .reshape(2, span_rows, width_local)
    )
    kernel_base = banded(filters.astype(jnp.float32))

    def advance(total, block_index):
        which_slot = block_index // blocks
        within = block_index % blocks * tap_count
        window = lax.dynamic_slice(
            extended, (which_slot, within, 0), (1, 2 * tap_count, width_local)
        )[0]
        rows_grad = lax.dynamic_slice(grad_c, (which_slot, within, 0), (1, tap_count, width_local))[
            0
        ]
        rows_offset = lax.dynamic_slice(doc_offset, (which_slot, within), (1, tap_count))[0]
        keep = band_mask(rows_offset, tap_count)
        kernel = kernel_base * keep[None]
        window_f = window.astype(jnp.float32).reshape(2 * tap_count, groups_local, group_width)
        grad_f = rows_grad.astype(jnp.float32).reshape(tap_count, groups_local, group_width)
        conv_rows = jnp.einsum("gij,jgc->igc", kernel, window_f, precision=exact).reshape(
            tap_count, width_local
        )
        spread = jnp.einsum("gij,igc->jgc", kernel, grad_f, precision=exact).reshape(
            2 * tap_count, width_local
        )
        products = jnp.einsum("igc,jgc->gij", grad_f, window_f, precision=exact)
        total = total + diagonals(products * keep[None])
        return (total, (conv_rows, spread[:tap_count], spread[tap_count:]))

    filter_total, (conv_blocks, spill_rows, own_rows) = lax.scan(
        advance,
        jnp.zeros((groups_local, tap_count), jnp.float32),
        jnp.arange(2 * blocks, dtype=jnp.int32),
    )
    conv_out = conv_blocks.reshape(tok_ctx, width_local)
    spill_rows = spill_rows.reshape(2, blocks, tap_count, width_local)
    own_rows = own_rows.reshape(2, blocks, tap_count, width_local)
    head_rows = jnp.concatenate([grad_c[0, :tap_count], grad_c[1, :tap_count]], axis=0)
    received = extended_2(head_rows, (("ctx", 0),), tap_count)
    head_first = jnp.where(last_rank, grad_c[1, :tap_count], received[3 * tap_count :])
    head_second = received[:tap_count]
    tap_ids = jnp.arange(tap_count, dtype=jnp.int32)
    next_first = (ctx_rank + 1) * span_rows + tap_ids
    next_second = (2 * n_ctx - ctx_rank) * span_rows + tap_ids

    def pull_back(head_grad, head_pos):
        kernel = kernel_base * band_mask(doc_reach(head_pos, doc_lens), tap_count)[None]
        return spread_back(kernel, head_grad, groups_local, group_width)[:tap_count]

    spill_first = pull_back(head_first, next_first)
    spill_second = pull_back(head_second, next_second)
    following = jnp.concatenate(
        [spill_rows[:, 1:], jnp.stack([spill_first, spill_second])[:, None]], axis=1
    )
    grad_h = (own_rows + following).reshape(tok_ctx, width_local)
    grad_q = (grad_y * conv_out).astype(jnp.bfloat16)
    grad_k = (grad_h * values.astype(jnp.float32)).astype(jnp.bfloat16)
    grad_v = (grad_h * key_in.astype(jnp.float32)).astype(jnp.bfloat16)
    grad_qkv = jnp.stack([grad_q, grad_k, grad_v])
    grad_scale = 1.0 / math.sqrt(tokens)
    grad_filters = lax.psum(filter_total, "ctx") * grad_scale
    gated = (queries.astype(jnp.float32) * conv_out).astype(jnp.bfloat16)
    grad_w = lax.psum_scatter(
        lax.dot_general(
            full_cot, gated, (((0,), (0,)), ((), ())), preferred_element_type=jnp.float32
        ),
        "ctx",
        scatter_dimension=0,
        tiled=True,
    )
    return (grad_qkv, grad_filters, grad_w * grad_scale)


def solution(mesh):
    return jax.shard_map(
        local,
        mesh=mesh,
        in_specs=(P(None, "ctx", "tp"), P("tp", None), P(None, "tp"), P(("ctx", "tp"), None), P()),
        out_specs=(P(None, "ctx", "tp"), P("tp", None), P("ctx", "tp")),
        check_vma=False,
    )
```

profile of v0, /device:TPU:4, one launch (start us, length us, event | category | flops | bytes accessed | tf_op | source)
XLA Modules:
  0.0 393.8 jit_solution(11501874476775541881)
XLA Ops:
  7.9 1.4 fusion.24
  9.4 3.5 collective-permute-start
  12.9 8.1 %collective-permute-start.1 = (bf16[128,1024]{1,0:T(8,128)(2,1)S(1)}, bf16[128,1024]{1,0:T(8,128)(2,1)S(1)}, u32[]{:S(2)}, u32[]{:S(2)}) collective-permute-start(bf16[128,1024]{1,0:T(8,128)(2,1)S(1)} %get-tuple-element.242), channel_id=1, source_target_pairs={{4,0},{8,4},{12,8},{16,12},{20,16},{24,20},{28,24},{32,28},{36,32}... | collective-permute-start | bytes 786440 | tf_op jit(solution)/shard_map/ppermute | solution.py:19
  24.3 5.4 %broadcast_in_dim.69 = f32[64,128,257]{2,1,0:T(8,128)} broadcast(f32[64,257]{1,0:T(8,128)S(1)} %maximum_maximum_fusion), dimensions={0,2} | broadcast | bytes 8487168 | tf_op jit(solution)/shard_map/broadcast_in_dim | solution.py:32
  29.6 12.4 %reshape.244 = f32[64,32896]{1,0:T(8,128)} reshape(f32[64,128,257]{2,1,0:T(8,128)} %broadcast_in_dim.69) | data formatting | bytes 16842752 | tf_op jit(solution)/shard_map/reshape | solution.py:32
  42.0 3.4 slice-done
  45.4 5.8 %copy.37 = f32[8,8,128,256]{3,2,1,0:T(8,128)} copy(f32[8,8,128,256]{3,1,2,0:T(8,128)S(1)} %bitcast.101) | data formatting | bytes 16777216
  51.3 7.4 %fusion.26 = (bf16[256,1024]{1,0:T(8,128)(2,1)S(1)}, f32[256,1024]{1,0:T(8,128)}) fusion(bf16[3,256,1024]{2,1,0:T(8,128)(2,1)} %param.7, bf16[256,4096]{1,0:T(8,128)(2,1)} %all-gather.2.cloned.1.call-done, bf16[4096,1024]{1,0:T(8,128)(2,1)} %param.9), kind=kOutput, calls=%fused_computation.36 | convolution fusion | flops 2148270080 | bytes 12582912 | tf_op jit(solution)/shard_map/dot_general | solution.py:88
  58.7 90.4 %while.19 = (s32[]{:T(128)}, f32[64,128]{1,0:T(8,128)}, f32[2,128,1024]{2,1,0:T(8,128)}, f32[2,128,1024]{1,2,0:T(8,128)}, s32[2]{0:T(128)S(1)}, /*index=5*/bf16[...) while((s32[]{:T(128)}, f32[64,128]{1,0:T(8,128)}, ...), condition=%wide.region_5.6_spmd.clone, body=%wide.region_3.5_spmd.clone.sunk | while | flops 879894528 | bytes 99649336 | solution.py:120
  61.7 6.4 %fusion.63 = f32[64,16,128]{2,1,0:T(8,128)S(1)} fusion(bf16[256,64,16]{0,2,1:T(8,128)(2,1)S(1)} %bitcast.95, f32[64,128,256]{2,1,0:T(8,128)} %get-tuple-element.336, f32[128,256]{1,0:T(8,128)S(1)} %fusion.62), kind=kOutput, calls=%fused_computation.2.clone.1 | convolution fusion | flops 404750336 | bytes 9568256 | tf_op jit(solution)/shard_map/while/body/eval_jaxpr/gij,jgc->igc/dot_general | solution.py:110
  69.2 5.4 %fusion.64 = f32[256,64,16]{0,2,1:T(8,128)S(1)} fusion(bf16[128,64,16]{0,2,1:T(8,128)(2,1)S(1)} %bitcast.97, f32[64,128,256]{2,1,0:T(8,128)} %get-tuple-element.336, f32[128,256]{1,0:T(8,128)S(1)} %fusion.62), kind=kOutput, calls=%fused_computation.8.clone.1 | convolution fusion | flops 404750336 | bytes 9830400 | tf_op jit(solution)/shard_map/while/body/eval_jaxpr/gij,igc->jgc/dot_general | solution.py:113
  76.0 4.7 %copy.44 = f32[8,8,128,256]{3,1,2,0:T(8,128)S(1)} copy(f32[8,8,128,256]{3,2,1,0:T(8,128)S(1)} %bitcast.93) | data formatting | bytes 16777216 | tf_op jit(solution)/shard_map/while
  80.7 3.8 pad.34
  84.5 14.2 %reshape.258 = f32[64,128,257]{2,1,0:T(8,128)} reshape(f32[64,32896]{1,0:T(8,128)} %pad.34) | data formatting | bytes 16842752 | tf_op jit(solution)/shard_map/while/body/eval_jaxpr/reshape | solution.py:41
  98.7 4.5 %slice_reduce_fusion.2 = f32[64,128]{1,0:T(8,128)S(1)} fusion(f32[64,128,257]{2,1,0:T(8,128)} %reshape.258), kind=kLoop, calls=%fused_computation.4.clone.1 | loop fusion | flops 1040384 | bytes 4227072 | tf_op jit(solution)/shard_map/while/body/eval_jaxpr/reduce_sum | solution.py:42
  106.9 6.4 %fusion.63 = f32[64,16,128]{2,1,0:T(8,128)S(1)} fusion(bf16[256,64,16]{0,2,1:T(8,128)(2,1)S(1)} %bitcast.95, f32[64,128,256]{2,1,0:T(8,128)} %get-tuple-element.336, f32[128,256]{1,0:T(8,128)S(1)} %fusion.62), kind=kOutput, calls=%fused_computation.2.clone.1 | convolution fusion | flops 404750336 | bytes 9568256 | tf_op jit(solution)/shard_map/while/body/eval_jaxpr/gij,jgc->igc/dot_general | solution.py:110
  114.4 5.4 %fusion.64 = f32[256,64,16]{0,2,1:T(8,128)S(1)} fusion(bf16[128,64,16]{0,2,1:T(8,128)(2,1)S(1)} %bitcast.97, f32[64,128,256]{2,1,0:T(8,128)} %get-tuple-element.336, f32[128,256]{1,0:T(8,128)S(1)} %fusion.62), kind=kOutput, calls=%fused_computation.8.clone.1 | convolution fusion | flops 404750336 | bytes 9830400 | tf_op jit(solution)/shard_map/while/body/eval_jaxpr/gij,igc->jgc/dot_general | solution.py:113
  121.2 4.7 %copy.44 = f32[8,8,128,256]{3,1,2,0:T(8,128)S(1)} copy(f32[8,8,128,256]{3,2,1,0:T(8,128)S(1)} %bitcast.93) | data formatting | bytes 16777216 | tf_op jit(solution)/shard_map/while
  126.0 3.8 pad.34
  129.7 14.2 %reshape.258 = f32[64,128,257]{2,1,0:T(8,128)} reshape(f32[64,32896]{1,0:T(8,128)} %pad.34) | data formatting | bytes 16842752 | tf_op jit(solution)/shard_map/while/body/eval_jaxpr/reshape | solution.py:41
  143.9 4.5 %slice_reduce_fusion.2 = f32[64,128]{1,0:T(8,128)S(1)} fusion(f32[64,128,257]{2,1,0:T(8,128)} %reshape.258), kind=kLoop, calls=%fused_computation.4.clone.1 | loop fusion | flops 1040384 | bytes 4227072 | tf_op jit(solution)/shard_map/while/body/eval_jaxpr/reduce_sum | solution.py:42
  149.1 2.8 fusion.27
  151.9 9.7 %convolution_bitcast_fusion = f32[4096,1024]{0,1:T(8,128)} fusion(bf16[256,1024]{1,0:T(8,128)(2,1)S(1)} %get-tuple-element.237, bf16[256,4096]{1,0:T(8,128)(2,1)} %all-gather.2.cloned.1.call-done), kind=kOutput, calls=%fused_computation.18 | convolution fusion | flops 2147483648 | bytes 19398656 | tf_op jit(solution)/shard_map/dot_general | solution.py:154
  162.4 2.5 collective-permute-start.2
  164.9 183.8 %psum.7 = f32[64,128]{1,0:T(8,128)S(1)} all-reduce(f32[64,128]{1,0:T(8,128)S(1)} %copy-done.5), channel_id=1, replica_groups=mesh['ctx'=32,'tp'=4] {'ctx'}, use_global_device_ids=true, to_apply=%region_8.9 | all-reduce | flops 8192 | bytes 65536 | tf_op jit(solution)/shard_map/psum | solution.py:151
  349.6 1.9 collective-permute-start.3
  351.5 5.4 %fusion.17 = f32[256,64,16]{0,2,1:T(8,128)S(1)} fusion(bf16[128,64,16]{0,2,1:T(8,128)(2,1)S(1)} %bitcast.110, f32[64,128,256]{2,1,0:T(8,128)} %get-tuple-element.343, f32[128,256]{1,0:T(8,128)S(1)} %fusion.31), kind=kOutput, calls=%fused_computation.26 | convolution fusion | flops 404750336 | bytes 9830400 | tf_op jit(solution)/shard_map/gij,igc->jgc/dot_general | solution.py:60
  357.8 10.8 %collective-permute-done.3 = bf16[128,1024]{1,0:T(8,128)(2,1)S(1)} collective-permute-done((bf16[128,1024]{1,0:T(8,128)(2,1)S(1)}, bf16[128,1024]{1,0:T(8,128)(2,1)S(1)}, u32[]{:S(2)}, u32[]{:S(2)}) %collective-permute-start.3) | collective-permute-done | bytes 262176 | tf_op jit(solution)/shard_map/ppermute | solution.py:17
  368.8 5.5 %fusion.20 = f32[256,64,16]{0,2,1:T(8,128)S(1)} fusion(bf16[128,64,16]{0,2,1:T(8,128)(2,1)S(1)} %bitcast.111, f32[64,128,256]{2,1,0:T(8,128)} %get-tuple-element.343, f32[128,256]{1,0:T(8,128)S(1)} %fusion.32), kind=kOutput, calls=%fused_computation.27 | convolution fusion | flops 404750336 | bytes 9830400 | tf_op jit(solution)/shard_map/gij,igc->jgc/dot_general | solution.py:60
  374.4 1.4 maximum_add_fusion
  377.1 1.5 fusion.25
  380.0 4.9 %reduce-scatter.2.cloned.1.call-done = f32[128,1024]{0,1:T(8,128)} async-done(((f32[4096,1024]{0,1:T(8,128)}), f32[128,1024]{0,1:T(8,128)}) %reduce-scatter.2.cloned.1.call-update) | async-done | bytes 524304 | tf_op jit(solution)/shard_map/reduce_scatter | solution.py:153
  (103 shorter events, 20.0 us)
Async XLA Ops:
  7.2 44.1 %all-gather.2.cloned.1.call-start = ((), (), s32[]{:S(2)}) async-start(), calls=%async_computation.1 | async-start | bytes 2621440 | tf_op jit(solution)/shard_map/all_gather | solution.py:87
  7.9 376.9 %reduce-scatter.2.cloned.1.call-start = ((), (), s32[]{:S(2)}) async-start(), calls=%async_computation.2 | async-start | bytes 17301504 | tf_op jit(solution)/shard_map/reduce_scatter | solution.py:153
  9.4 41.8 %collective-permute-start = (bf16[128,1024]{1,0:T(8,128)(2,1)S(1)}, bf16[128,1024]{1,0:T(8,128)(2,1)S(1)}, u32[]{:S(2)}, u32[]{:S(2)}) collective-permute-start(bf16[128,1024]{1,0:T(8,128)(2,1)S(1)} %get-tuple-element.241), channel_id=1, source_target_pairs={{0,4},{4,8},{8,12},{12,16},{16,20},{20,24},{24,28},{28,32},{32,36}... | collective-permute-start | bytes 786440 | tf_op jit(solution)/shard_map/ppermute | solution.py:17
  12.9 38.3 %collective-permute-start.1 = (bf16[128,1024]{1,0:T(8,128)(2,1)S(1)}, bf16[128,1024]{1,0:T(8,128)(2,1)S(1)}, u32[]{:S(2)}, u32[]{:S(2)}) collective-permute-start(bf16[128,1024]{1,0:T(8,128)(2,1)S(1)} %get-tuple-element.242), channel_id=1, source_target_pairs={{4,0},{8,4},{12,8},{16,12},{20,16},{24,20},{28,24},{32,28},{36,32}... | collective-permute-start | bytes 786440 | tf_op jit(solution)/shard_map/ppermute | solution.py:19
  42.0 3.4 slice-start
  68.3 6.3 %copy-start.6 = (f32[2,128,1024]{1,2,0:T(8,128)S(1)}, f32[2,128,1024]{1,2,0:T(8,128)}, u32[]{:S(2)}) copy-start(f32[2,128,1024]{1,2,0:T(8,128)} %get-tuple-element.318) | copy-start | bytes 3145732 | tf_op jit(solution)/shard_map/while
  74.7 1.3 copy-start.7
  84.5 18.8 %copy-start.3 = (f32[64,128]{1,0:T(8,128)S(1)}, f32[64,128]{1,0:T(8,128)}, u32[]{:S(2)}) copy-start(f32[64,128]{1,0:T(8,128)} %get-tuple-element.316) | copy-start | bytes 98308 | tf_op jit(solution)/shard_map/while
  103.3 0.6 copy-start.4
  113.6 6.3 %copy-start.6 = (f32[2,128,1024]{1,2,0:T(8,128)S(1)}, f32[2,128,1024]{1,2,0:T(8,128)}, u32[]{:S(2)}) copy-start(f32[2,128,1024]{1,2,0:T(8,128)} %get-tuple-element.318) | copy-start | bytes 3145732 | tf_op jit(solution)/shard_map/while
  119.9 1.3 copy-start.7
  129.7 18.8 %copy-start.3 = (f32[64,128]{1,0:T(8,128)S(1)}, f32[64,128]{1,0:T(8,128)}, u32[]{:S(2)}) copy-start(f32[64,128]{1,0:T(8,128)} %get-tuple-element.316) | copy-start | bytes 98308 | tf_op jit(solution)/shard_map/while
  148.5 0.6 copy-start.4
  161.6 0.6 copy-start.9
  161.6 0.6 copy-start.8
  161.6 3.3 copy-start.5
  162.4 187.0 %collective-permute-start.2 = (bf16[128,1024]{1,0:T(8,128)(2,1)S(1)}, bf16[128,1024]{1,0:T(8,128)(2,1)S(1)}, u32[]{:S(2)}, u32[]{:S(2)}) collective-permute-start(bf16[128,1024]{1,0:T(8,128)(2,1)S(1)} %slice.80), channel_id=1, source_target_pairs={{4,0},{8,4},{12,8},{16,12},{20,16},{24,20},{28,24},{32,28},{36,32}... | collective-permute-start | bytes 786440 | tf_op jit(solution)/shard_map/ppermute | solution.py:19
  349.6 19.0 %collective-permute-start.3 = (bf16[128,1024]{1,0:T(8,128)(2,1)S(1)}, bf16[128,1024]{1,0:T(8,128)(2,1)S(1)}, u32[]{:S(2)}, u32[]{:S(2)}) collective-permute-start(bf16[128,1024]{1,0:T(8,128)(2,1)S(1)} %get-tuple-element.240), channel_id=1, source_target_pairs={{0,4},{4,8},{8,12},{12,16},{16,20},{20,24},{24,28},{28,32},{32,36}... | collective-permute-start | bytes 786440 | tf_op jit(solution)/shard_map/ppermute | solution.py:17
  357.8 19.3 %copy-start = (bf16[3,256,1024]{2,1,0:T(8,128)(2,1)S(1)}, bf16[3,256,1024]{2,1,0:T(8,128)(2,1)}, u32[]{:S(2)}) copy-start(bf16[3,256,1024]{2,1,0:T(8,128)(2,1)} %param.7) | copy-start | bytes 4718596
  368.8 5.6 %copy-start.2 = (f32[128,64,16]{0,2,1:T(8,128)S(1)}, f32[128,64,16]{0,2,1:T(8,128)}, u32[]{:S(2)}) copy-start(f32[128,64,16]{0,2,1:T(8,128)} %slice.81) | copy-start | bytes 1572868
  368.8 9.9 %copy-start.1 = (bf16[256,1024]{1,0:T(8,128)(2,1)S(1)}, bf16[256,1024]{1,0:T(8,128)(2,1)}, u32[]{:S(2)}) copy-start(bf16[256,1024]{1,0:T(8,128)(2,1)} %get-tuple-element.238) | copy-start | bytes 1572868
Sparse Core Ops, SparseCore 0:
  9.7 35.2 all-gather.1
  161.8 223.0 reduce-scatter.1
where the time goes:
time: 395 us; the launch traced here: 394 us
  blocking collectives  184 us (47%)
  local copies, waits for them, and re-layouts  83.7 us (21%)
  matrix products  54.2 us (14%)
  other arithmetic  21.3 us (5%)
  waiting for transfers between devices  16.4 us (4%)
  starting transfers between devices  16 us (4%)
  between operations  14.3 us (4%)
  loops' own time  3.97 us (1%)
    psum x1, blocking collectives, local(): grad_filters = lax.psum(filter_total, 'ctx') * grad_scale  184 us
    reshape x2, local copies, waits for them, and re-layouts, diagonals(): flattened.reshape(groups, tap_count, width + 1)[:, :, 1:tap_count + 1]  28.3 us
    dot_general x2, matrix products, advance(): jnp.einsum('gij,jgc->igc', kernel, window_f, precision=exact)  12.8 us
    reshape x1, local copies, waits for them, and re-layouts, banded(): jnp.broadcast_to(pattern[:, None, :], (groups, tap_count, width + 1))  12.4 us
    dot_general x2, matrix products, spread_back(): jnp.einsum('gij,igc->jgc', kernel, grad_f, precision=lax.Precision.HIGHEST)  11 us
    ppermute x2, waiting for transfers between devices, extended_2(): lax.ppermute(tail, axis, [(i, (i + 1) % count) for i in range(ends)])  10.8 us
    dot_general x2, matrix products, advance(): jnp.einsum('gij,igc->jgc', kernel, grad_f, precision=exact)  10.7 us
    while x18, local copies, waits for them, and re-layouts  10.7 us
  transfers between devices with their start and end apart: 6, of which 2 were waited for; matrix products, arithmetic and copies ran while one was open for 12% of the time, Pallas kernels for 0%

commit v1 on v0

v1 whole, which is shorter than its diff:
```python
import functools
import math

import jax
import jax.numpy as jnp
from jax import lax
from jax.experimental import pallas as pl
from jax.experimental.pallas import tpu as pltpu
from jax.sharding import PartitionSpec as P

F32 = jnp.float32
BF16 = jnp.bfloat16
MESH = pl.DeviceIdType.MESH
BIG = 64 * 1024 * 1024 - 65536
SPAN = 128
LANES = 128


def doc_starts_row(doc_ref, pos):
    def step(d, carry):
        start, best = carry
        best = jnp.where(pos >= start, start, best)
        return start + doc_ref[d], best

    return lax.fori_loop(0, doc_ref.shape[0], step, (jnp.int32(0), jnp.zeros_like(pos)))[1]


def as_column(row):
    return jnp.broadcast_to(row.astype(F32), (LANES, LANES)).T.astype(jnp.int32)


def sheared(padded, base_ref):
    groups = padded.shape[0]
    for r in range(8):
        turned = padded if r == 0 else pltpu.roll(padded, r, 1)
        for n in range(2):
            base_ref[n, pl.ds(r, groups, stride=8), :] = turned[:, n * LANES : (n + 1) * LANES]


def toeplitz(base_ref, out_ref):
    def one(g, carry):
        rows = pl.ds(pl.multiple_of(g * 8, 8), 8)
        slab = jnp.concatenate([base_ref[0, rows, :], base_ref[1, rows, :]], axis=1)
        for q in range(0, 16, 2):
            low = slab if q == 0 else pltpu.roll(slab, 8 * q, 1)
            high = pltpu.roll(slab, 8 * q + 8, 1)
            out_ref[g, 8 * q : 8 * q + 16, :] = jnp.concatenate([low, high], axis=0).astype(BF16)
        return carry

    lax.fori_loop(0, out_ref.shape[0], one, 0)


def flipped(filters):
    row = lax.broadcasted_iota(jnp.int32, (LANES, LANES), 0)
    col = lax.broadcasted_iota(jnp.int32, (LANES, LANES), 1)
    anti = (row + col == LANES - 1).astype(F32).astype(BF16)
    return jnp.dot(filters, anti, preferred_element_type=F32)


def block_position(slot, rank, count):
    return (rank if slot == 0 else 2 * count - 1 - rank) * SPAN


def window_mask(doc_ref, start):
    lane = lax.broadcasted_iota(jnp.int32, (1, LANES), 1)
    begins = as_column(doc_starts_row(doc_ref, lane + start))
    begins = jnp.concatenate([begins, begins], axis=1)
    col = lax.broadcasted_iota(jnp.int32, (SPAN, 2 * SPAN), 1) + (start - SPAN)
    return (col >= begins).astype(jnp.int32)


def spread_mask(doc_ref, start, next_start):
    lane = lax.broadcasted_iota(jnp.int32, (1, LANES), 1)
    begins = jnp.concatenate(
        [doc_starts_row(doc_ref, lane + start), doc_starts_row(doc_ref, lane + next_start)], axis=1
    )
    row = lax.broadcasted_iota(jnp.int32, (SPAN, 2 * SPAN), 0) + start
    return (row >= jnp.broadcast_to(begins, (SPAN, 2 * SPAN))).astype(jnp.int32)


def conv_kernel(count, doc_ref, filt_ref, qkv_ref, prev_ref, c_ref, yt_ref, base, toep, mask, win):
    rank = lax.axis_index("ctx")
    flip = flipped(filt_ref[...])
    sheared(pltpu.roll(jnp.concatenate([flip, jnp.zeros_like(flip)], axis=1), 1, 1), base)
    toeplitz(base, toep)
    for slot in range(2):
        mask[slot] = (
            window_mask(doc_ref, block_position(slot, rank, count)).astype(F32).astype(BF16)
        )
        win[slot, :SPAN] = prev_ref[slot]
        rows = slice(slot * SPAN, (slot + 1) * SPAN)
        win[slot, SPAN:] = (qkv_ref[1, rows].astype(F32) * qkv_ref[2, rows].astype(F32)).astype(
            BF16
        )
    owner = lax.broadcasted_iota(jnp.int32, (SPAN, LANES), 1) // 16
    tiles = c_ref.shape[1] // LANES

    def tile(n, carry):
        slot, t = n // tiles, n % tiles
        cols = pl.ds(pl.multiple_of(t * LANES, LANES), LANES)
        rows = pl.ds(pl.multiple_of(slot * SPAN, SPAN), SPAN)
        window = win[slot, :, cols]
        keep = mask[slot]
        total = jnp.zeros((SPAN, LANES), F32)
        for u in range(8):
            part = jnp.dot(toep[t * 8 + u] * keep, window, preferred_element_type=F32)
            total = jnp.where(owner == u, part, total)
        c_ref[rows, cols] = total
        gated = (qkv_ref[0, rows, cols].astype(F32) * total).astype(BF16).astype(F32)
        yt_ref[cols, rows] = gated.T.astype(BF16)
        return carry

    lax.fori_loop(0, 2 * tiles, tile, 0)


def conv_call(doc_lens, filters, qkv, prev, count):
    groups = filters.shape[0]
    width = qkv.shape[2]
    return pl.pallas_call(
        functools.partial(conv_kernel, count),
        out_shape=(
            jax.ShapeDtypeStruct((2 * SPAN, width), F32),
            jax.ShapeDtypeStruct((width, 2 * SPAN), BF16),
        ),
        in_specs=[pl.BlockSpec(memory_space=pltpu.SMEM)]
        + [pl.BlockSpec(memory_space=pltpu.VMEM)] * 3,
        out_specs=(pl.BlockSpec(memory_space=pltpu.VMEM),) * 2,
        scratch_shapes=[
            pltpu.VMEM((2, 8 * groups, SPAN), F32),
            pltpu.VMEM((groups, SPAN, 2 * SPAN), BF16),
            pltpu.VMEM((2, SPAN, 2 * SPAN), BF16),
            pltpu.VMEM((2, 2 * SPAN, width), BF16),
        ],
        compiler_params=pltpu.CompilerParams(vmem_limit_bytes=40 * 1024 * 1024),
        name="conv",
    )(doc_lens, filters, qkv, prev)


def back_kernel(
    count,
    doc_ref,
    filt_ref,
    qkv_ref,
    prev_ref,
    dc_ref,
    dcn_ref,
    gq_ref,
    out_ref,
    gf_ref,
    base,
    toep,
    spread,
    keep,
    win,
    dwin,
    diag,
):
    rank = lax.axis_index("ctx")
    filt = filt_ref[...].astype(F32)
    sheared(jnp.concatenate([filt, jnp.zeros_like(filt)], axis=1), base)
    toeplitz(base, toep)
    out_ref[0] = gq_ref[...]
    for slot in range(2):
        start = block_position(slot, rank, count)
        follow = (rank + 1) * SPAN if slot == 0 else (2 * count - rank) * SPAN
        keep[slot] = window_mask(doc_ref, start).astype(F32)
        spread[slot] = spread_mask(doc_ref, start, follow).astype(F32).astype(BF16)
        rows = slice(slot * SPAN, (slot + 1) * SPAN)
        win[slot, :SPAN] = prev_ref[slot]
        win[slot, SPAN:] = (qkv_ref[1, rows].astype(F32) * qkv_ref[2, rows].astype(F32)).astype(
            BF16
        )
        dwin[slot, :SPAN] = dc_ref[rows]
        dwin[slot, SPAN:] = dcn_ref[slot]
    owner = lax.broadcasted_iota(jnp.int32, (SPAN, LANES), 1) // 16
    tiles = dc_ref.shape[1] // LANES

    def tile(n, carry):
        slot, t = n // tiles, n % tiles
        cols = pl.ds(pl.multiple_of(t * LANES, LANES), LANES)
        rows = pl.ds(pl.multiple_of(slot * SPAN, SPAN), SPAN)
        window = dwin[slot, :, cols]
        mask = spread[slot]
        total = jnp.zeros((SPAN, LANES), F32)
        for u in range(8):
            part = jnp.dot(toep[t * 8 + u] * mask, window, preferred_element_type=F32)
            total = jnp.where(owner == u, part, total)
        out_ref[1, rows, cols] = (total * qkv_ref[2, rows, cols].astype(F32)).astype(BF16)
        out_ref[2, rows, cols] = (total * qkv_ref[1, rows, cols].astype(F32)).astype(BF16)
        return carry

    lax.fori_loop(0, 2 * tiles, tile, 0)

    def taps(t, carry):
        cols = pl.ds(pl.multiple_of(t * LANES, LANES), LANES)
        for u in range(8):
            both = None
            for slot in range(2):
                grad = dwin[slot, :SPAN, cols].astype(F32)
                grad = jnp.where(owner == u, grad, 0.0).astype(BF16)
                prod = lax.dot_general(
                    grad, win[slot, :, cols], (((1,), (1,)), ((), ())), preferred_element_type=F32
                )
                prod = prod * keep[slot]
                both = prod if both is None else both + prod
            slabs = [both[8 * q : 8 * q + 8] for q in range(16)]
            while len(slabs) > 1:
                half = len(slabs) // 2
                slabs = [
                    slabs[q] + pltpu.roll(slabs[q + half], 2 * SPAN - 8 * half, 1)
                    for q in range(half)
                ]
            rows = pl.ds(pl.multiple_of(t * 64 + u * 8, 8), 8)
            diag[0, rows, :] = slabs[0][:, :LANES]
            diag[1, rows, :] = slabs[0][:, LANES:]
        return carry

    lax.fori_loop(0, tiles, taps, 0)
    groups = gf_ref.shape[0]
    total = None
    for r in range(8):
        row = jnp.concatenate([diag[n, pl.ds(r, groups, stride=8), :] for n in range(2)], axis=1)
        total = row if r == 0 else total + pltpu.roll(row, 2 * SPAN - r, 1)
    gf_ref[...] = pltpu.roll(total, 2 * SPAN - 1, 1)[:, :LANES]


def back_call(doc_lens, filters, qkv, prev, dc, dcn, gq, count):
    groups = filters.shape[0]
    width = qkv.shape[2]
    return pl.pallas_call(
        functools.partial(back_kernel, count),
        out_shape=(
            jax.ShapeDtypeStruct(qkv.shape, BF16),
            jax.ShapeDtypeStruct((groups, LANES), F32),
        ),
        in_specs=[pl.BlockSpec(memory_space=pltpu.SMEM)]
        + [pl.BlockSpec(memory_space=pltpu.VMEM)] * 6,
        out_specs=(pl.BlockSpec(memory_space=pltpu.VMEM),) * 2,
        scratch_shapes=[
            pltpu.VMEM((2, 8 * groups, SPAN), F32),
            pltpu.VMEM((groups, SPAN, 2 * SPAN), BF16),
            pltpu.VMEM((2, SPAN, 2 * SPAN), BF16),
            pltpu.VMEM((2, SPAN, 2 * SPAN), F32),
            pltpu.VMEM((2, 2 * SPAN, width), BF16),
            pltpu.VMEM((2, 2 * SPAN, width), BF16),
            pltpu.VMEM((2, 8 * groups, SPAN), F32),
        ],
        compiler_params=pltpu.CompilerParams(vmem_limit_bytes=40 * 1024 * 1024),
        name="back",
    )(doc_lens, filters, qkv, prev, dc, dcn, gq)


def project_kernel(
    scale,
    cot_ref,
    yt_ref,
    w_ref,
    qkv_ref,
    c_ref,
    gw_ref,
    dc_ref,
    gq_ref,
    full,
    w_v,
    q_v,
    part,
    relay1,
    done1,
    red,
    relay2,
    done2,
    away,
    kept,
    far,
    load_sem,
    cot_send,
    cot_recv,
    send1,
    recv1,
    send2,
    recv2,
    far_send,
    far_recv,
):
    ctx = lax.axis_index("ctx")
    tp = lax.axis_index("tp")
    my_y = ctx % 4
    my_z = (ctx // 4) % 4
    my_x = ctx // 16
    place = (my_y, my_z)
    stride = (1, 4)
    rows_local = cot_ref.shape[0]

    def around(axis, step):
        return ctx + stride[axis] * ((place[axis] + step) % 4 - place[axis])

    across = ctx + 16 - 32 * my_x
    core = tp + 1 - 2 * (tp % 2)
    beside = tp + 2 - 4 * (tp // 2)

    barrier = pltpu.get_barrier_semaphore()
    for axis in range(2):
        for step in (1, 3):
            pl.semaphore_signal(
                barrier, inc=1, device_id=(around(axis, step), tp), device_id_type=MESH
            )
    pl.semaphore_signal(barrier, inc=1, device_id=(across, tp), device_id_type=MESH)
    pl.semaphore_signal(barrier, inc=1, device_id=(ctx, core), device_id_type=MESH)
    pl.semaphore_signal(barrier, inc=1, device_id=(ctx, beside), device_id_type=MESH)
    load_w = pltpu.make_async_copy(w_ref, w_v, load_sem.at[0])
    load_q = pltpu.make_async_copy(qkv_ref.at[0], q_v, load_sem.at[1])
    pl.semaphore_wait(barrier, 7)

    half_cols = cot_ref.shape[1] // 2
    col0 = [
        pl.multiple_of((1 - my_x) * half_cols, half_cols),
        pl.multiple_of(my_x * half_cols, half_cols),
    ]

    def cot_copy(k, n, src, owner, target):
        rows = pl.ds(pl.multiple_of(owner * rows_local, rows_local), rows_local)
        cols = pl.ds(col0[k], half_cols)
        return pltpu.make_async_remote_copy(
            src_ref=cot_ref.at[:, cols] if src is None else full.at[rows, cols],
            dst_ref=full.at[rows, cols],
            send_sem=cot_send.at[k, n],
            recv_sem=cot_recv.at[k, n],
            device_id=(ctx, target),
            device_id_type=MESH,
        )

    side = [cot_copy(k, 0, None, tp, beside) for k in range(2)]
    near = [cot_copy(k, 1, None, tp, core) for k in range(2)]
    pass_on = [cot_copy(k, 2, full, beside, core) for k in range(2)]
    for k in range(2):
        side[k].start()
        near[k].start()
    load_w.start()
    load_q.start()
    full[pl.ds(pl.multiple_of(tp * rows_local, rows_local), rows_local), :] = cot_ref[...]

    def gather(k):
        side[k].wait_recv()
        pass_on[k].start()
        near[k].wait_recv()
        pass_on[k].wait_recv()

    def partial(k):
        def block(i, carry):
            tokens = full[:, pl.ds(pl.multiple_of(col0[k] + i * 256, 256), 256)]

            def some(m, inner):
                rows = pl.ds(pl.multiple_of(m * 256, 256), 256)
                out = jnp.dot(yt_ref[rows, :], tokens, preferred_element_type=F32).astype(BF16)
                part[k, i // 2, (i % 2) * 2, rows, :] = out[:, :LANES]
                part[k, i // 2, (i % 2) * 2 + 1, rows, :] = out[:, LANES:]
                return inner

            return lax.fori_loop(0, 4, some, carry)

        lax.fori_loop(0, 8, block, 0)

    def quarter(axis, half):
        first = axis * 512 + half * 256
        return slice(first, first + 256)

    def piece1(axis, k, j, half):
        if axis == 0:
            return part.at[k, :, j, quarter(axis, half)]
        return part.at[k, j, :, quarter(axis, half)]

    def piece2(axis, k, j, half):
        return red.at[axis, k, j, pl.ds(half * 256, 256)]

    def ring(stage, axis, k):
        ring_axis = axis if stage == 1 else 1 - axis
        m = place[ring_axis]
        up, down = around(ring_axis, 1), around(ring_axis, 3)
        piece = piece1 if stage == 1 else piece2
        relays = relay1 if stage == 1 else relay2
        done = done1 if stage == 1 else done2
        send, recv = (send1, recv1) if stage == 1 else (send2, recv2)
        nxt, prv, opp = (m + 1) % 4, (m + 3) % 4, (m + 2) % 4
        table = [
            (piece(axis, k, opp, 0), relays.at[axis, k, 0], up),
            (piece(axis, k, opp, 1), relays.at[axis, k, 1], down),
            (piece(axis, k, nxt, 1), done.at[axis, k, 0], up),
            (piece(axis, k, prv, 0), done.at[axis, k, 1], down),
            (piece(axis, k, nxt, 0), done.at[axis, k, 2], up),
            (piece(axis, k, prv, 1), done.at[axis, k, 3], down),
        ]
        copies = [
            pltpu.make_async_remote_copy(
                src_ref=src,
                dst_ref=dst,
                send_sem=send.at[axis, k, n],
                recv_sem=recv.at[axis, k, n],
                device_id=(target, tp),
                device_id_type=MESH,
            )
            for n, (src, dst, target) in enumerate(table)
        ]

        def start():
            for n in range(4):
                copies[n].start()

        def forward():
            for n in range(2):
                copies[n].wait_recv()
                mine = piece(axis, k, nxt if n == 0 else prv, n)
                mine[...] = (mine[...].astype(F32) + relays[axis, k, n].astype(F32)).astype(BF16)
                copies[4 + n].start()

        def finish(half):
            copies[3 if half == 0 else 2].wait_recv()
            copies[4 if half == 0 else 5].wait_recv()
            total = piece(axis, k, m, half)[...].astype(F32)
            total = total + done[axis, k, 1 if half == 0 else 0].astype(F32)
            return total + done[axis, k, 2 if half == 0 else 3].astype(F32)

        return start, forward, finish, copies

    first = [[ring(1, axis, k) for axis in range(2)] for k in range(2)]
    second = [[ring(2, axis, k) for axis in range(2)] for k in range(2)]

    for k in range(2):
        gather(k)
        partial(k)
        for axis in range(2):
            first[k][axis][0]()

    load_w.wait()
    load_q.wait()

    def project(n, carry):
        cols = pl.ds(pl.multiple_of(n * 256, 256), 256)
        dy = jnp.dot(full[...], w_v[:, cols], preferred_element_type=F32)
        dc_ref[:, cols] = (q_v[:, cols].astype(F32) * dy).astype(BF16)
        gq_ref[:, cols] = (dy * c_ref[:, cols]).astype(BF16)
        return carry

    lax.fori_loop(0, 4, project, 0)

    for k in range(2):
        for axis in range(2):
            first[k][axis][1]()
    for k in range(2):
        for axis in range(2):
            for half in range(2):
                red[axis, k, :, half * 256 : half * 256 + 256, :] = first[k][axis][2](half).astype(
                    BF16
                )
            second[k][axis][0]()
    for k in range(2):
        for axis in range(2):
            second[k][axis][1]()
    for k in range(2):
        for axis in range(2):
            for half in range(2):
                total = second[k][axis][2](half)
                if k == 0:
                    away[quarter(axis, half)] = total.astype(BF16)
                else:
                    kept[quarter(axis, half)] = total
        if k == 0:
            over = pltpu.make_async_remote_copy(
                src_ref=away,
                dst_ref=far,
                send_sem=far_send,
                recv_sem=far_recv,
                device_id=(across, tp),
                device_id_type=MESH,
            )
            over.start()
    over.wait_recv()
    for n in range(8):
        rows = slice(n * LANES, (n + 1) * LANES)
        gw_ref[:, rows] = ((kept[rows] + far[rows].astype(F32)) * scale).T
    over.wait_send()
    for k in range(2):
        side[k].wait_send()
        near[k].wait_send()
        pass_on[k].wait_send()
        for axis in range(2):
            for copy in first[k][axis][3] + second[k][axis][3]:
                copy.wait_send()


def project_call(cot, yt, w_out, qkv, c, scale):
    rows_local, feats = cot.shape
    width = w_out.shape[1]
    tokens = qkv.shape[1]
    vm = pl.BlockSpec(memory_space=pltpu.VMEM)
    hb = pl.BlockSpec(memory_space=pl.ANY)
    return pl.pallas_call(
        functools.partial(project_kernel, scale),
        out_shape=(
            jax.ShapeDtypeStruct((feats // 32, width), F32),
            jax.ShapeDtypeStruct((tokens, width), BF16),
            jax.ShapeDtypeStruct((tokens, width), BF16),
        ),
        in_specs=[vm, vm, hb, hb, vm],
        out_specs=(vm, vm, vm),
        scratch_shapes=[
            pltpu.VMEM((tokens, feats), BF16),
            pltpu.VMEM((feats, width), BF16),
            pltpu.VMEM((tokens, width), BF16),
            pltpu.VMEM((2, 4, 4, width, LANES), BF16),
            pltpu.VMEM((2, 2, 2, 4, 256, LANES), BF16),
            pltpu.VMEM((2, 2, 4, 4, 256, LANES), BF16),
            pltpu.VMEM((2, 2, 4, 512, LANES), BF16),
            pltpu.VMEM((2, 2, 2, 256, LANES), BF16),
            pltpu.VMEM((2, 2, 4, 256, LANES), BF16),
            pltpu.VMEM((width, LANES), BF16),
            pltpu.VMEM((width, LANES), F32),
            pltpu.VMEM((width, LANES), BF16),
            pltpu.SemaphoreType.DMA((2,)),
            pltpu.SemaphoreType.DMA((2, 3)),
            pltpu.SemaphoreType.DMA((2, 3)),
            pltpu.SemaphoreType.DMA((2, 2, 6)),
            pltpu.SemaphoreType.DMA((2, 2, 6)),
            pltpu.SemaphoreType.DMA((2, 2, 6)),
            pltpu.SemaphoreType.DMA((2, 2, 6)),
            pltpu.SemaphoreType.DMA,
            pltpu.SemaphoreType.DMA,
        ],
        compiler_params=pltpu.CompilerParams(
            vmem_limit_bytes=60 * 1024 * 1024, collective_id=0, has_side_effects=True
        ),
        name="project",
    )(cot, yt, w_out, qkv, c)


def neighbours(low, high, count):
    ahead = lax.ppermute(low, "ctx", [(i, i + 1) for i in range(count - 1)])
    behind = lax.ppermute(high, "ctx", [(i + 1, i) for i in range(count - 1)])
    return ahead, behind


def local(qkv, filters, w_out, cotangent, doc_lens):
    count = lax.axis_size("ctx")
    last = lax.axis_index("ctx") == count - 1
    tokens = qkv.shape[1] * count
    scale = 1.0 / math.sqrt(tokens)
    hidden = (qkv[1].astype(F32) * qkv[2].astype(F32)).astype(BF16)
    before, after = neighbours(hidden[:SPAN], hidden[SPAN:], count)
    prev = jnp.stack([before, jnp.where(last, hidden[:SPAN], after)])
    conv, gated = conv_call(doc_lens, filters, qkv, prev, count)
    grad_w, grad_c, grad_q = project_call(cotangent, gated, w_out, qkv, conv, scale)
    before, after = neighbours(grad_c[SPAN:], grad_c[:SPAN], count)
    follow = jnp.stack([jnp.where(last, grad_c[SPAN:], after), before])
    grad_qkv, taps = back_call(doc_lens, filters, qkv, prev, grad_c, follow, grad_q, count)
    taps = lax.psum(taps, "ctx")
    return grad_qkv, jnp.flip(taps, axis=1) * scale, grad_w


def solution(mesh):
    return jax.shard_map(
        local,
        mesh=mesh,
        in_specs=(P(None, "ctx", "tp"), P("tp", None), P(None, "tp"), P(("ctx", "tp"), None), P()),
        out_specs=(P(None, "ctx", "tp"), P("tp", None), P("ctx", "tp")),
        check_vma=False,
    )
```

time: 395 us -> 345 us (0.87)
  Pallas kernels: 0 us -> 106 us
  local copies, waits for them, and re-layouts: 83.7 us -> 3.82 us
  matrix products: 54.2 us -> 0 us
  other arithmetic: 21.3 us -> 3.16 us
  waiting for transfers between devices: 16.4 us -> 33.2 us
  between operations: 14.3 us -> 0.83 us
  blocking collectives: 184 us -> 178 us
  loops' own time: 3.97 us -> 0 us
    pallas_call x0 -> x3, Pallas kernels: none -> 106 us  [the longest x1 71.5 us: project_call(): pl.pallas_call(functools.partial(project_kernel, scale), out_shape=(jax.S...]
    dot_general x10 -> x0, matrix products: 54.2 us -> none  [the longest x2 12.8 us: advance(): jnp.einsum('gij,jgc->igc', kernel, window_f, precision=exact)]
    reshape x3 -> x0, local copies, waits for them, and re-layouts: 40.7 us -> none  [the longest x2 28.3 us: diagonals(): flattened.reshape(groups, tap_count, width + 1)[:, :, 1:tap_count + 1]]
    ppermute x4, waiting for transfers between devices: 10.8 us -> 33.2 us  [the longest x2 23.8 us: neighbours(): ahead = lax.ppermute(low, 'ctx', [(i, i + 1) for i in range(count - 1)])]
    while x18 -> x0, local copies, waits for them, and re-layouts: 10.7 us -> none
    reduce_sum x2 -> x0, other arithmetic: 9.07 us -> none  [diagonals(): return jnp.flip(jnp.sum(sheared, axis=1), axis=1)]
    pad x2 -> x0, local copies, waits for them, and re-layouts: 7.5 us -> none  [diagonals(): jnp.pad(products.reshape(groups, tap_count * width), ((0, 0), (0, tap_cou...]
    psum x1, blocking collectives: 184 us -> 178 us  [local(): taps = lax.psum(taps, 'ctx')]
  transfers between devices with their start and end apart: 6 -> 4, of which waited for: 2 -> 4; matrix products, arithmetic and copies ran while one was open for 12% -> 0% of each run, Pallas kernels for 0% -> 0%
where the time goes in v1:
time: 345 us; the launch traced here: 344 us
  blocking collectives  178 us (52%)
  Pallas kernels  106 us (31%)
  waiting for transfers between devices  33.2 us (10%)
  starting transfers between devices  19.9 us (6%)
  local copies, waits for them, and re-layouts  3.82 us (1%)
    psum x1, blocking collectives, local(): taps = lax.psum(taps, 'ctx')  178 us
    pallas_call x1, Pallas kernels, project_call(): pl.pallas_call(functools.partial(project_kernel, scale), out_shape=(jax.S...  71.5 us
    ppermute x2, waiting for transfers between devices, neighbours(): ahead = lax.ppermute(low, 'ctx', [(i, i + 1) for i in range(count - 1)])  23.8 us
    pallas_call x1, Pallas kernels, back_call(): pl.pallas_call(functools.partial(back_kernel, count), out_shape=(jax.Shap...  20.5 us
    ppermute x2, starting transfers between devices, neighbours(): behind = lax.ppermute(high, 'ctx', [(i + 1, i) for i in range(count - 1)])  16.1 us
    pallas_call x1, Pallas kernels, conv_call(): pl.pallas_call(functools.partial(conv_kernel, count), out_shape=(jax.Shap...  13.6 us
    ppermute x2, waiting for transfers between devices, neighbours(): behind = lax.ppermute(high, 'ctx', [(i + 1, i) for i in range(count - 1)])  9.46 us
  transfers between devices with their start and end apart: 4, of which 4 were waited for; matrix products, arithmetic and copies ran while one was open for 0% of the time, Pallas kernels for 0%

profile of v1, /device:TPU:4, one launch (start us, length us, event | category | flops | bytes accessed | tf_op | source)
XLA Modules:
  0.0 344.4 jit_solution(4020738506862635764)
XLA Ops:
  0.6 1.4 multiply_convert_fusion
  2.0 0.0 copy-start
  2.0 0.0 copy-start.6
  2.1 0.0 copy-start.7
  2.1 8.5 %collective-permute-start.1 = (bf16[128,1024]{1,0:T(8,128)(2,1)S(1)}, bf16[128,1024]{1,0:T(8,128)(2,1)S(1)}, u32[]{:S(2)}, u32[]{:S(2)}) collective-permute-start(bf16[128,1024]{1,0:T(8,128)(2,1)S(1)} %get-tuple-element.20), channel_id=1, source_target_pairs={{4,0},{8,4},{12,8},{16,12},{20,16},{24,20},{28,24},{32,28},{36,32}... | collective-permute-start | bytes 786440 | tf_op jit(solution)/shard_map/ppermute | solution.py:537
  10.6 1.9 collective-permute-start
  12.5 3.6 %collective-permute-done.1 = bf16[128,1024]{1,0:T(8,128)(2,1)S(1)} collective-permute-done((bf16[128,1024]{1,0:T(8,128)(2,1)S(1)}, bf16[128,1024]{1,0:T(8,128)(2,1)S(1)}, u32[]{:S(2)}, u32[]{:S(2)}) %collective-permute-start.1) | collective-permute-done | bytes 262176 | tf_op jit(solution)/shard_map/ppermute | solution.py:537
  16.2 9.8 %collective-permute-done = bf16[128,1024]{1,0:T(8,128)(2,1)S(1)} collective-permute-done((bf16[128,1024]{1,0:T(8,128)(2,1)S(1)}, bf16[128,1024]{1,0:T(8,128)(2,1)S(1)}, u32[]{:S(2)}, u32[]{:S(2)}) %collective-permute-start) | collective-permute-done | bytes 262176 | tf_op jit(solution)/shard_map/ppermute | solution.py:536
  26.0 0.1 pad_maximum_fusion.prev_ref
  26.0 0.0 copy-done
  26.0 0.0 copy-done.6
  26.0 0.0 copy-done.7
  26.1 13.6 %conv.1 = (f32[256,1024]{1,0:T(8,128)S(1)}, bf16[1024,256]{1,0:T(8,128)(2,1)S(1)}) custom-call(s32[64]{0:T(128)S(1)} %copy-done.7, bf16[64,128]{1,0:T(8,128)(2,1)S(1)} %copy-done.6, bf16[3,256,1024]{2,1,0:T(8,128)(2,1)S(1)} %copy-done, bf16[2,128,1024]{2,1,0:T(8,128)(2,1)S(1)} %pad_maximum_fusion.prev_ref), custom_call_target="tpu_custom_call" | custom-call | tf_op jit(solution)/shard_map/conv/pallas_call | solution.py:119
  39.7 0.0 copy-start.3
  39.7 1.0 copy-done.3
  40.7 0.8 copy-done.4
  41.5 71.5 %project.1 = (f32[128,1024]{1,0:T(8,128)}, bf16[256,1024]{1,0:T(8,128)(2,1)}, bf16[256,1024]{1,0:T(8,128)(2,1)}) custom-call(bf16[64,4096]{1,0:T(8,128)(2,1)} %cot_ref.1, bf16[1024,256]{1,0:T(8,128)(2,1)} %copy-done.4, bf16[4096,1024]{1,0:T(8,128)(2,1)} %w_ref.1, bf16[3,256,1024]{2,1,0:T(8,128)(2,1)} %qkv_ref.5, f32[256,1024]{1,0:T(8,128)} %copy-done.3), custom_call_target="tpu_custom_call" | custom-call | tf_op jit(solution)/shard_map/project/pallas_call | solution.py:496
  112.9 0.0 copy-start.1
  112.9 0.0 copy-start.2
  112.9 0.0 copy-start.5
  113.0 1.1 slice.33
  114.1 7.6 %collective-permute-start.2 = (bf16[128,1024]{1,0:T(8,128)(2,1)S(1)}, bf16[128,1024]{1,0:T(8,128)(2,1)S(1)}, u32[]{:S(2)}, u32[]{:S(2)}) collective-permute-start(bf16[128,1024]{1,0:T(8,128)(2,1)S(1)} %slice.33), channel_id=1, source_target_pairs={{4,0},{8,4},{12,8},{16,12},{20,16},{24,20},{28,24},{32,28},{36,32}... | collective-permute-start | bytes 786440 | tf_op jit(solution)/shard_map/ppermute | solution.py:537
  121.7 5.9 %collective-permute-done.2 = bf16[128,1024]{1,0:T(8,128)(2,1)S(1)} collective-permute-done((bf16[128,1024]{1,0:T(8,128)(2,1)S(1)}, bf16[128,1024]{1,0:T(8,128)(2,1)S(1)}, u32[]{:S(2)}, u32[]{:S(2)}) %collective-permute-start.2) | collective-permute-done | bytes 262176 | tf_op jit(solution)/shard_map/ppermute | solution.py:537
  127.6 1.0 select_bitcast_fusion
  128.6 1.9 collective-permute-start.3
  130.5 14.0 %collective-permute-done.3 = bf16[128,1024]{1,0:T(8,128)(2,1)S(1)} collective-permute-done((bf16[128,1024]{1,0:T(8,128)(2,1)S(1)}, bf16[128,1024]{1,0:T(8,128)(2,1)S(1)}, u32[]{:S(2)}, u32[]{:S(2)}) %collective-permute-start.3) | collective-permute-done | bytes 262176 | tf_op jit(solution)/shard_map/ppermute | solution.py:536
  144.5 0.1 pad_maximum_fusion.1.dcn_ref
  144.5 20.5 %back.1 = (bf16[3,256,1024]{2,1,0:T(8,128)(2,1)}, f32[64,128]{1,0:T(8,128)S(1)}) custom-call(s32[64]{0:T(128)S(1)} %copy-done.7, bf16[64,128]{1,0:T(8,128)(2,1)S(1)} %copy-done.6, bf16[3,256,1024]{2,1,0:T(8,128)(2,1)S(1)} %copy-done.1, bf16[2,128,1024]{2,1,0:T(8,128)(2,1)S(1)} %pad_maximum_fusion.prev_ref, bf16[256,1024]{1,0:T(8,128)(2,1)S(1)} %copy-done.2, ...), custom_call_target="tpu_custom_call" | custom-call | tf_op jit(solution)/shard_map/back/pallas_call | solution.py:230
  165.1 0.1 rev.4
  165.2 177.9 %psum.7 = f32[64,128]{1,0:T(8,128)S(1)} all-reduce(f32[64,128]{1,0:T(8,128)S(1)} %rev.4), channel_id=1, replica_groups=mesh['ctx'=32,'tp'=4] {'ctx'}, use_global_device_ids=true, to_apply=%region_0.1 | all-reduce | flops 8192 | bytes 65536 | tf_op jit(solution)/shard_map/psum | solution.py:554
  343.0 0.6 broadcast_multiply_fusion
  343.6 0.8 copy.9
  (8 shorter events, 0.1 us)
Async XLA Ops:
  2.0 24.0 %copy-start = (bf16[3,256,1024]{2,1,0:T(8,128)(2,1)S(1)}, bf16[3,256,1024]{2,1,0:T(8,128)(2,1)}, u32[]{:S(2)}) copy-start(bf16[3,256,1024]{2,1,0:T(8,128)(2,1)} %qkv_ref.5) | copy-start | bytes 4718596
  2.0 24.0 %copy-start.6 = (bf16[64,128]{1,0:T(8,128)(2,1)S(1)}, bf16[64,128]{1,0:T(8,128)(2,1)}, u32[]{:S(2)}) copy-start(bf16[64,128]{1,0:T(8,128)(2,1)} %filt_ref.3) | copy-start | bytes 49156
  2.1 24.0 %copy-start.7 = (s32[64]{0:T(128)S(1)}, s32[64]{0:T(128)}, u32[]{:S(2)}) copy-start(s32[64]{0:T(128)} %doc_ref.3) | copy-start | bytes 772
  2.1 14.0 %collective-permute-start.1 = (bf16[128,1024]{1,0:T(8,128)(2,1)S(1)}, bf16[128,1024]{1,0:T(8,128)(2,1)S(1)}, u32[]{:S(2)}, u32[]{:S(2)}) collective-permute-start(bf16[128,1024]{1,0:T(8,128)(2,1)S(1)} %get-tuple-element.20), channel_id=1, source_target_pairs={{4,0},{8,4},{12,8},{16,12},{20,16},{24,20},{28,24},{32,28},{36,32}... | collective-permute-start | bytes 786440 | tf_op jit(solution)/shard_map/ppermute | solution.py:537
  10.6 15.4 %collective-permute-start = (bf16[128,1024]{1,0:T(8,128)(2,1)S(1)}, bf16[128,1024]{1,0:T(8,128)(2,1)S(1)}, u32[]{:S(2)}, u32[]{:S(2)}) collective-permute-start(bf16[128,1024]{1,0:T(8,128)(2,1)S(1)} %get-tuple-element.19), channel_id=1, source_target_pairs={{0,4},{4,8},{8,12},{12,16},{16,20},{20,24},{24,28},{28,32},{32,36}... | collective-permute-start | bytes 786440 | tf_op jit(solution)/shard_map/ppermute | solution.py:536
  39.7 1.0 copy-start.3
  40.7 0.8 copy-start.4
  112.9 31.6 %copy-start.1 = (bf16[3,256,1024]{2,1,0:T(8,128)(2,1)S(1)}, bf16[3,256,1024]{2,1,0:T(8,128)(2,1)}, u32[]{:S(2)}) copy-start(bf16[3,256,1024]{2,1,0:T(8,128)(2,1)} %qkv_ref.5) | copy-start | bytes 4718596
  112.9 31.6 %copy-start.2 = (bf16[256,1024]{1,0:T(8,128)(2,1)S(1)}, bf16[256,1024]{1,0:T(8,128)(2,1)}, u32[]{:S(2)}) copy-start(bf16[256,1024]{1,0:T(8,128)(2,1)} %get-tuple-element.12.dc_ref) | copy-start | bytes 1572868
  112.9 31.6 %copy-start.5 = (bf16[256,1024]{1,0:T(8,128)(2,1)S(1)}, bf16[256,1024]{1,0:T(8,128)(2,1)}, u32[]{:S(2)}) copy-start(bf16[256,1024]{1,0:T(8,128)(2,1)} %get-tuple-element.13.gq_ref) | copy-start | bytes 1572868
  114.1 13.5 %collective-permute-start.2 = (bf16[128,1024]{1,0:T(8,128)(2,1)S(1)}, bf16[128,1024]{1,0:T(8,128)(2,1)S(1)}, u32[]{:S(2)}, u32[]{:S(2)}) collective-permute-start(bf16[128,1024]{1,0:T(8,128)(2,1)S(1)} %slice.33), channel_id=1, source_target_pairs={{4,0},{8,4},{12,8},{16,12},{20,16},{24,20},{28,24},{32,28},{36,32}... | collective-permute-start | bytes 786440 | tf_op jit(solution)/shard_map/ppermute | solution.py:537
  128.6 15.9 %collective-permute-start.3 = (bf16[128,1024]{1,0:T(8,128)(2,1)S(1)}, bf16[128,1024]{1,0:T(8,128)(2,1)S(1)}, u32[]{:S(2)}, u32[]{:S(2)}) collective-permute-start(bf16[128,1024]{1,0:T(8,128)(2,1)S(1)} %get-tuple-element.18), channel_id=1, source_target_pairs={{0,4},{4,8},{8,12},{12,16},{16,20},{20,24},{24,28},{28,32},{32,36}... | collective-permute-start | bytes 786440 | tf_op jit(solution)/shard_map/ppermute | solution.py:536
  144.5 199.1 %copy-start.8 = (f32[128,1024]{1,0:T(8,128)S(1)}, f32[128,1024]{1,0:T(8,128)}, u32[]{:S(2)}) copy-start(f32[128,1024]{1,0:T(8,128)} %get-tuple-element.26) | copy-start | bytes 1572868

commit v2 on v1

--- a/solution.py
+++ b/solution.py
@@ -154,8 +154,26 @@
     win,
     dwin,
     diag,
+    tap_y,
+    tap_z,
+    tap_x,
+    tap_send,
+    tap_recv,
 ):
     rank = lax.axis_index("ctx")
+    tp = lax.axis_index("tp")
+    place = (rank % 4, (rank // 4) % 4)
+    across = rank + 16 - 32 * (rank // 16)
+
+    def around(axis, step):
+        return rank + (1, 4)[axis] * ((place[axis] + step) % 4 - place[axis])
+
+    partners = [[around(axis, step) for step in (1, 2, 3)] for axis in range(2)] + [[across]]
+    barrier = pltpu.get_barrier_semaphore()
+    for targets in partners:
+        for target in targets:
+            pl.semaphore_signal(barrier, inc=1, device_id=(target, tp), device_id_type=MESH)
+    pl.semaphore_wait(barrier, 7)
     filt = filt_ref[...].astype(F32)
     sheared(jnp.concatenate([filt, jnp.zeros_like(filt)], axis=1), base)
     toeplitz(base, toep)
@@ -221,7 +239,34 @@
     for r in range(8):
         row = jnp.concatenate([diag[n, pl.ds(r, groups, stride=8), :] for n in range(2)], axis=1)
         total = row if r == 0 else total + pltpu.roll(row, 2 * SPAN - r, 1)
-    gf_ref[...] = pltpu.roll(total, 2 * SPAN - 1, 1)[:, :LANES]
+    total = pltpu.roll(total, 2 * SPAN - 1, 1)[:, :LANES]
+
+    copies = []
+    for n, buffer in enumerate((tap_y, tap_z, tap_x)):
+        buffer[0] = total
+        sent = [
+            pltpu.make_async_remote_copy(
+                src_ref=buffer.at[0],
+                dst_ref=buffer.at[i + 1],
+                send_sem=tap_send.at[n, i],
+                recv_sem=tap_recv.at[n, i],
+                device_id=(target, tp),
+                device_id_type=MESH,
+            )
+            for i, target in enumerate(partners[n])
+        ]
+        for copy in sent:
+            copy.start()
+        for copy in sent:
+            copy.wait_recv()
+        if n < 2:
+            total = (buffer[0] + buffer[2]) + (buffer[1] + buffer[3])
+        else:
+            total = buffer[0] + buffer[1]
+        copies += sent
+    gf_ref[...] = total
+    for copy in copies:
+        copy.wait_send()
 
 
 def back_call(doc_lens, filters, qkv, prev, dc, dcn, gq, count):
@@ -244,8 +289,15 @@
             pltpu.VMEM((2, 2 * SPAN, width), BF16),
             pltpu.VMEM((2, 2 * SPAN, width), BF16),
             pltpu.VMEM((2, 8 * groups, SPAN), F32),
+            pltpu.VMEM((4, groups, LANES), F32),
+            pltpu.VMEM((4, groups, LANES), F32),
+            pltpu.VMEM((2, groups, LANES), F32),
+            pltpu.SemaphoreType.DMA((3, 3)),
+            pltpu.SemaphoreType.DMA((3, 3)),
         ],
-        compiler_params=pltpu.CompilerParams(vmem_limit_bytes=40 * 1024 * 1024),
+        compiler_params=pltpu.CompilerParams(
+            vmem_limit_bytes=40 * 1024 * 1024, collective_id=1, has_side_effects=True
+        ),
         name="back",
     )(doc_lens, filters, qkv, prev, dc, dcn, gq)
 
@@ -551,7 +603,6 @@
     before, after = neighbours(grad_c[SPAN:], grad_c[:SPAN], count)
     follow = jnp.stack([jnp.where(last, grad_c[SPAN:], after), before])
     grad_qkv, taps = back_call(doc_lens, filters, qkv, prev, grad_c, follow, grad_q, count)
-    taps = lax.psum(taps, "ctx")
     return grad_qkv, jnp.flip(taps, axis=1) * scale, grad_w
 
 

time: 345 us -> 182 us (0.53)
  blocking collectives: 178 us -> 0 us
  Pallas kernels: 106 us -> 117 us
    psum x1 -> x0, blocking collectives: 178 us -> none  [local(): taps = lax.psum(taps, 'ctx')]
    pallas_call x1, Pallas kernels: 20.5 us -> 31.4 us  [back_call(): pl.pallas_call(functools.partial(back_kernel, count), out_shape=(jax.Shap...]
where the time goes in v2:
time: 182 us; the launch traced here: 179 us
  Pallas kernels  117 us (64%)
  waiting for transfers between devices  33.2 us (18%)
  starting transfers between devices  19.9 us (11%)
  local copies, waits for them, and re-layouts  5.21 us (3%)
  other arithmetic  3.17 us (2%)
    pallas_call x1, Pallas kernels, project_call(): pl.pallas_call(functools.partial(project_kernel, scale), out_shape=(jax.S...  71.5 us
    pallas_call x1, Pallas kernels, back_call(): pl.pallas_call(functools.partial(back_kernel, count), out_shape=(jax.Shap...  31.4 us
    ppermute x2, waiting for transfers between devices, neighbours(): ahead = lax.ppermute(low, 'ctx', [(i, i + 1) for i in range(count - 1)])  23.8 us
    ppermute x2, starting transfers between devices, neighbours(): behind = lax.ppermute(high, 'ctx', [(i + 1, i) for i in range(count - 1)])  16.1 us
    pallas_call x1, Pallas kernels, conv_call(): pl.pallas_call(functools.partial(conv_kernel, count), out_shape=(jax.Shap...  13.6 us
    ppermute x2, waiting for transfers between devices, neighbours(): behind = lax.ppermute(high, 'ctx', [(i + 1, i) for i in range(count - 1)])  9.46 us
    unnamed x20, local copies, waits for them, and re-layouts  3.98 us
    ppermute x2, starting transfers between devices, neighbours(): ahead = lax.ppermute(low, 'ctx', [(i, i + 1) for i in range(count - 1)])  3.84 us
  transfers between devices with their start and end apart: 4, of which 4 were waited for; matrix products, arithmetic and copies ran while one was open for 0% of the time, Pallas kernels for 0%

profile of v2, /device:TPU:4, one launch (start us, length us, event | category | flops | bytes accessed | tf_op | source)
XLA Modules:
  0.0 178.9 jit_solution(10331146864606284833)
XLA Ops:
  0.6 1.4 multiply_convert_fusion
  2.0 0.0 copy-start
  2.0 0.0 copy-start.6
  2.1 0.0 copy-start.7
  2.1 8.5 %collective-permute-start.1 = (bf16[128,1024]{1,0:T(8,128)(2,1)S(1)}, bf16[128,1024]{1,0:T(8,128)(2,1)S(1)}, u32[]{:S(2)}, u32[]{:S(2)}) collective-permute-start(bf16[128,1024]{1,0:T(8,128)(2,1)S(1)} %get-tuple-element.20), channel_id=1, source_target_pairs={{4,0},{8,4},{12,8},{16,12},{20,16},{24,20},{28,24},{32,28},{36,32}... | collective-permute-start | bytes 786440 | tf_op jit(solution)/shard_map/ppermute | solution.py:589
  10.6 1.9 %collective-permute-start = (bf16[128,1024]{1,0:T(8,128)(2,1)S(1)}, bf16[128,1024]{1,0:T(8,128)(2,1)S(1)}, u32[]{:S(2)}, u32[]{:S(2)}) collective-permute-start(bf16[128,1024]{1,0:T(8,128)(2,1)S(1)} %get-tuple-element.19), channel_id=1, source_target_pairs={{0,4},{4,8},{8,12},{12,16},{16,20},{20,24},{24,28},{28,32},{32,36}... | collective-permute-start | bytes 786440 | tf_op jit(solution)/shard_map/ppermute | solution.py:588
  12.5 3.6 %collective-permute-done.1 = bf16[128,1024]{1,0:T(8,128)(2,1)S(1)} collective-permute-done((bf16[128,1024]{1,0:T(8,128)(2,1)S(1)}, bf16[128,1024]{1,0:T(8,128)(2,1)S(1)}, u32[]{:S(2)}, u32[]{:S(2)}) %collective-permute-start.1) | collective-permute-done | bytes 262176 | tf_op jit(solution)/shard_map/ppermute | solution.py:589
  16.2 9.8 %collective-permute-done = bf16[128,1024]{1,0:T(8,128)(2,1)S(1)} collective-permute-done((bf16[128,1024]{1,0:T(8,128)(2,1)S(1)}, bf16[128,1024]{1,0:T(8,128)(2,1)S(1)}, u32[]{:S(2)}, u32[]{:S(2)}) %collective-permute-start) | collective-permute-done | bytes 262176 | tf_op jit(solution)/shard_map/ppermute | solution.py:588
  26.0 0.1 pad_maximum_fusion.prev_ref
  26.0 0.0 copy-done
  26.0 0.0 copy-done.6
  26.1 13.6 %conv.1 = (f32[256,1024]{1,0:T(8,128)S(1)}, bf16[1024,256]{1,0:T(8,128)(2,1)S(1)}) custom-call(s32[64]{0:T(128)S(1)} %copy-done.7, bf16[64,128]{1,0:T(8,128)(2,1)S(1)} %copy-done.6, bf16[3,256,1024]{2,1,0:T(8,128)(2,1)S(1)} %copy-done, bf16[2,128,1024]{2,1,0:T(8,128)(2,1)S(1)} %pad_maximum_fusion.prev_ref), custom_call_target="tpu_custom_call" | custom-call | tf_op jit(solution)/shard_map/conv/pallas_call | solution.py:119
  39.7 0.0 copy-start.3
  39.7 1.0 copy-done.3
  40.7 0.8 copy-done.4
  41.5 71.5 %project.1 = (f32[128,1024]{1,0:T(8,128)}, bf16[256,1024]{1,0:T(8,128)(2,1)}, bf16[256,1024]{1,0:T(8,128)(2,1)}) custom-call(bf16[64,4096]{1,0:T(8,128)(2,1)} %cot_ref.1, bf16[1024,256]{1,0:T(8,128)(2,1)} %copy-done.4, bf16[4096,1024]{1,0:T(8,128)(2,1)} %w_ref.1, bf16[3,256,1024]{2,1,0:T(8,128)(2,1)} %qkv_ref.5, f32[256,1024]{1,0:T(8,128)} %copy-done.3), custom_call_target="tpu_custom_call" | custom-call | tf_op jit(solution)/shard_map/project/pallas_call | solution.py:548
  112.9 0.0 copy-start.1
  113.0 0.0 copy-start.2
  113.0 0.0 copy-start.5
  113.0 1.1 slice.33
  114.1 7.6 %collective-permute-start.2 = (bf16[128,1024]{1,0:T(8,128)(2,1)S(1)}, bf16[128,1024]{1,0:T(8,128)(2,1)S(1)}, u32[]{:S(2)}, u32[]{:S(2)}) collective-permute-start(bf16[128,1024]{1,0:T(8,128)(2,1)S(1)} %slice.33), channel_id=1, source_target_pairs={{4,0},{8,4},{12,8},{16,12},{20,16},{24,20},{28,24},{32,28},{36,32}... | collective-permute-start | bytes 786440 | tf_op jit(solution)/shard_map/ppermute | solution.py:589
  121.7 5.9 %collective-permute-done.2 = bf16[128,1024]{1,0:T(8,128)(2,1)S(1)} collective-permute-done((bf16[128,1024]{1,0:T(8,128)(2,1)S(1)}, bf16[128,1024]{1,0:T(8,128)(2,1)S(1)}, u32[]{:S(2)}, u32[]{:S(2)}) %collective-permute-start.2) | collective-permute-done | bytes 262176 | tf_op jit(solution)/shard_map/ppermute | solution.py:589
  127.6 1.0 select_bitcast_fusion
  128.6 1.9 %collective-permute-start.3 = (bf16[128,1024]{1,0:T(8,128)(2,1)S(1)}, bf16[128,1024]{1,0:T(8,128)(2,1)S(1)}, u32[]{:S(2)}, u32[]{:S(2)}) collective-permute-start(bf16[128,1024]{1,0:T(8,128)(2,1)S(1)} %get-tuple-element.18), channel_id=1, source_target_pairs={{0,4},{4,8},{8,12},{12,16},{16,20},{20,24},{24,28},{28,32},{32,36}... | collective-permute-start | bytes 786440 | tf_op jit(solution)/shard_map/ppermute | solution.py:588
  130.5 14.0 %collective-permute-done.3 = bf16[128,1024]{1,0:T(8,128)(2,1)S(1)} collective-permute-done((bf16[128,1024]{1,0:T(8,128)(2,1)S(1)}, bf16[128,1024]{1,0:T(8,128)(2,1)S(1)}, u32[]{:S(2)}, u32[]{:S(2)}) %collective-permute-start.3) | collective-permute-done | bytes 262176 | tf_op jit(solution)/shard_map/ppermute | solution.py:588
  144.5 0.1 pad_maximum_fusion.1.dcn_ref
  144.6 31.4 %back.1 = (bf16[3,256,1024]{2,1,0:T(8,128)(2,1)S(1)}, f32[64,128]{1,0:T(8,128)S(1)}) custom-call(s32[64]{0:T(128)S(1)} %copy-done.7, bf16[64,128]{1,0:T(8,128)(2,1)S(1)} %copy-done.6, bf16[3,256,1024]{2,1,0:T(8,128)(2,1)S(1)} %copy-done.1, bf16[2,128,1024]{2,1,0:T(8,128)(2,1)S(1)} %pad_maximum_fusion.prev_ref, bf16[256,1024]{1,0:T(8,128)(2,1)S(1)} %copy-done.2, ...), custom_call_target="tpu_custom_call" | custom-call | tf_op jit(solution)/shard_map/back/pallas_call | solution.py:275
  176.0 0.1 rev.4
  176.0 0.6 broadcast_multiply_fusion
  176.7 1.1 copy.10
  177.8 0.3 copy-done.8
  178.1 0.8 copy.11
  (8 shorter events, 0.1 us)
Async XLA Ops:
  2.0 24.0 %copy-start = (bf16[3,256,1024]{2,1,0:T(8,128)(2,1)S(1)}, bf16[3,256,1024]{2,1,0:T(8,128)(2,1)}, u32[]{:S(2)}) copy-start(bf16[3,256,1024]{2,1,0:T(8,128)(2,1)} %qkv_ref.5) | copy-start | bytes 4718596
  2.0 24.0 %copy-start.6 = (bf16[64,128]{1,0:T(8,128)(2,1)S(1)}, bf16[64,128]{1,0:T(8,128)(2,1)}, u32[]{:S(2)}) copy-start(bf16[64,128]{1,0:T(8,128)(2,1)} %filt_ref.3) | copy-start | bytes 49156
  2.1 24.0 %copy-start.7 = (s32[64]{0:T(128)S(1)}, s32[64]{0:T(128)}, u32[]{:S(2)}) copy-start(s32[64]{0:T(128)} %doc_ref.3) | copy-start | bytes 772
  2.1 14.0 %collective-permute-start.1 = (bf16[128,1024]{1,0:T(8,128)(2,1)S(1)}, bf16[128,1024]{1,0:T(8,128)(2,1)S(1)}, u32[]{:S(2)}, u32[]{:S(2)}) collective-permute-start(bf16[128,1024]{1,0:T(8,128)(2,1)S(1)} %get-tuple-element.20), channel_id=1, source_target_pairs={{4,0},{8,4},{12,8},{16,12},{20,16},{24,20},{28,24},{32,28},{36,32}... | collective-permute-start | bytes 786440 | tf_op jit(solution)/shard_map/ppermute | solution.py:589
  10.6 15.4 %collective-permute-start = (bf16[128,1024]{1,0:T(8,128)(2,1)S(1)}, bf16[128,1024]{1,0:T(8,128)(2,1)S(1)}, u32[]{:S(2)}, u32[]{:S(2)}) collective-permute-start(bf16[128,1024]{1,0:T(8,128)(2,1)S(1)} %get-tuple-element.19), channel_id=1, source_target_pairs={{0,4},{4,8},{8,12},{12,16},{16,20},{20,24},{24,28},{28,32},{32,36}... | collective-permute-start | bytes 786440 | tf_op jit(solution)/shard_map/ppermute | solution.py:588
  39.7 1.0 copy-start.3
  40.7 0.8 copy-start.4
  112.9 31.6 %copy-start.1 = (bf16[3,256,1024]{2,1,0:T(8,128)(2,1)S(1)}, bf16[3,256,1024]{2,1,0:T(8,128)(2,1)}, u32[]{:S(2)}) copy-start(bf16[3,256,1024]{2,1,0:T(8,128)(2,1)} %qkv_ref.5) | copy-start | bytes 4718596
  113.0 31.6 %copy-start.2 = (bf16[256,1024]{1,0:T(8,128)(2,1)S(1)}, bf16[256,1024]{1,0:T(8,128)(2,1)}, u32[]{:S(2)}) copy-start(bf16[256,1024]{1,0:T(8,128)(2,1)} %get-tuple-element.12.dc_ref) | copy-start | bytes 1572868
  113.0 31.6 %copy-start.5 = (bf16[256,1024]{1,0:T(8,128)(2,1)S(1)}, bf16[256,1024]{1,0:T(8,128)(2,1)}, u32[]{:S(2)}) copy-start(bf16[256,1024]{1,0:T(8,128)(2,1)} %get-tuple-element.13.gq_ref) | copy-start | bytes 1572868
  114.1 13.5 %collective-permute-start.2 = (bf16[128,1024]{1,0:T(8,128)(2,1)S(1)}, bf16[128,1024]{1,0:T(8,128)(2,1)S(1)}, u32[]{:S(2)}, u32[]{:S(2)}) collective-permute-start(bf16[128,1024]{1,0:T(8,128)(2,1)S(1)} %slice.33), channel_id=1, source_target_pairs={{4,0},{8,4},{12,8},{16,12},{20,16},{24,20},{28,24},{32,28},{36,32}... | collective-permute-start | bytes 786440 | tf_op jit(solution)/shard_map/ppermute | solution.py:589
  128.6 15.9 %collective-permute-start.3 = (bf16[128,1024]{1,0:T(8,128)(2,1)S(1)}, bf16[128,1024]{1,0:T(8,128)(2,1)S(1)}, u32[]{:S(2)}, u32[]{:S(2)}) collective-permute-start(bf16[128,1024]{1,0:T(8,128)(2,1)S(1)} %get-tuple-element.18), channel_id=1, source_target_pairs={{0,4},{4,8},{8,12},{12,16},{16,20},{20,24},{24,28},{28,32},{32,36}... | collective-permute-start | bytes 786440 | tf_op jit(solution)/shard_map/ppermute | solution.py:588
  176.7 1.4 copy-start.8

commit v3 on v2

--- a/solution.py
+++ b/solution.py
@@ -78,8 +78,51 @@
     return (row >= jnp.broadcast_to(begins, (SPAN, 2 * SPAN))).astype(jnp.int32)
 
 
-def conv_kernel(count, doc_ref, filt_ref, qkv_ref, prev_ref, c_ref, yt_ref, base, toep, mask, win):
+def halo_copies(sources, edge, targets, send, recv):
+    tp = lax.axis_index("tp")
+    return [
+        pltpu.make_async_remote_copy(
+            src_ref=sources[slot],
+            dst_ref=edge.at[slot],
+            send_sem=send.at[slot],
+            recv_sem=recv.at[slot],
+            device_id=(targets[slot], tp),
+            device_id_type=MESH,
+        )
+        for slot in range(2)
+    ]
+
+
+def conv_kernel(
+    count,
+    doc_ref,
+    filt_ref,
+    qkv_ref,
+    c_ref,
+    yt_ref,
+    win,
+    base,
+    toep,
+    mask,
+    own,
+    edge,
+    edge_send,
+    edge_recv,
+):
     rank = lax.axis_index("ctx")
+    ends = ((rank + 1) % count, (rank + count - 1) % count)
+    barrier = pltpu.get_barrier_semaphore()
+    for target in ends:
+        pl.semaphore_signal(
+            barrier, inc=1, device_id=(target, lax.axis_index("tp")), device_id_type=MESH
+        )
+    for slot in range(2):
+        rows = slice(slot * SPAN, (slot + 1) * SPAN)
+        own[slot] = (qkv_ref[1, rows].astype(F32) * qkv_ref[2, rows].astype(F32)).astype(BF16)
+    pl.semaphore_wait(barrier, 2)
+    halo = halo_copies([own.at[0], own.at[1]], edge, ends, edge_send, edge_recv)
+    for copy in halo:
+        copy.start()
     flip = flipped(filt_ref[...])
     sheared(pltpu.roll(jnp.concatenate([flip, jnp.zeros_like(flip)], axis=1), 1, 1), base)
     toeplitz(base, toep)
@@ -87,11 +130,11 @@
         mask[slot] = (
             window_mask(doc_ref, block_position(slot, rank, count)).astype(F32).astype(BF16)
         )
-        win[slot, :SPAN] = prev_ref[slot]
-        rows = slice(slot * SPAN, (slot + 1) * SPAN)
-        win[slot, SPAN:] = (qkv_ref[1, rows].astype(F32) * qkv_ref[2, rows].astype(F32)).astype(
-            BF16
-        )
+    for slot in range(2):
+        halo[slot].wait_recv()
+        win[slot, SPAN:] = own[slot]
+    win[0, :SPAN] = edge[0]
+    win[1, :SPAN] = jnp.where(rank == count - 1, own[0], edge[1])
     owner = lax.broadcasted_iota(jnp.int32, (SPAN, LANES), 1) // 16
     tiles = c_ref.shape[1] // LANES
 
@@ -111,9 +154,11 @@
         return carry
 
     lax.fori_loop(0, 2 * tiles, tile, 0)
-
-
-def conv_call(doc_lens, filters, qkv, prev, count):
+    for copy in halo:
+        copy.wait_send()
+
+
+def conv_call(doc_lens, filters, qkv, count):
     groups = filters.shape[0]
     width = qkv.shape[2]
     return pl.pallas_call(
@@ -121,19 +166,25 @@
         out_shape=(
             jax.ShapeDtypeStruct((2 * SPAN, width), F32),
             jax.ShapeDtypeStruct((width, 2 * SPAN), BF16),
+            jax.ShapeDtypeStruct((2, 2 * SPAN, width), BF16),
         ),
         in_specs=[pl.BlockSpec(memory_space=pltpu.SMEM)]
-        + [pl.BlockSpec(memory_space=pltpu.VMEM)] * 3,
-        out_specs=(pl.BlockSpec(memory_space=pltpu.VMEM),) * 2,
+        + [pl.BlockSpec(memory_space=pltpu.VMEM)] * 2,
+        out_specs=(pl.BlockSpec(memory_space=pltpu.VMEM),) * 3,
         scratch_shapes=[
             pltpu.VMEM((2, 8 * groups, SPAN), F32),
             pltpu.VMEM((groups, SPAN, 2 * SPAN), BF16),
             pltpu.VMEM((2, SPAN, 2 * SPAN), BF16),
-            pltpu.VMEM((2, 2 * SPAN, width), BF16),
+            pltpu.VMEM((2, SPAN, width), BF16),
+            pltpu.VMEM((2, SPAN, width), BF16),
+            pltpu.SemaphoreType.DMA((2,)),
+            pltpu.SemaphoreType.DMA((2,)),
         ],
-        compiler_params=pltpu.CompilerParams(vmem_limit_bytes=40 * 1024 * 1024),
+        compiler_params=pltpu.CompilerParams(
+            vmem_limit_bytes=40 * 1024 * 1024, collective_id=2, has_side_effects=True
+        ),
         name="conv",
-    )(doc_lens, filters, qkv, prev)
+    )(doc_lens, filters, qkv)
 
 
 def back_kernel(
@@ -141,9 +192,8 @@
     doc_ref,
     filt_ref,
     qkv_ref,
-    prev_ref,
+    win,
     dc_ref,
-    dcn_ref,
     gq_ref,
     out_ref,
     gf_ref,
@@ -151,14 +201,16 @@
     toep,
     spread,
     keep,
-    win,
     dwin,
+    edge,
     diag,
     tap_y,
     tap_z,
     tap_x,
     tap_send,
     tap_recv,
+    edge_send,
+    edge_recv,
 ):
     rank = lax.axis_index("ctx")
     tp = lax.axis_index("tp")
@@ -173,10 +225,19 @@
     for targets in partners:
         for target in targets:
             pl.semaphore_signal(barrier, inc=1, device_id=(target, tp), device_id_type=MESH)
-    pl.semaphore_wait(barrier, 7)
-    filt = filt_ref[...].astype(F32)
-    sheared(jnp.concatenate([filt, jnp.zeros_like(filt)], axis=1), base)
-    toeplitz(base, toep)
+    ends = ((rank + count - 1) % count, (rank + 1) % count)
+    for target in ends:
+        pl.semaphore_signal(barrier, inc=1, device_id=(target, tp), device_id_type=MESH)
+    pl.semaphore_wait(barrier, 9)
+    halo = halo_copies(
+        [dc_ref.at[slot * SPAN : (slot + 1) * SPAN] for slot in range(2)],
+        edge,
+        ends,
+        edge_send,
+        edge_recv,
+    )
+    for copy in halo:
+        copy.start()
     out_ref[0] = gq_ref[...]
     for slot in range(2):
         start = block_position(slot, rank, count)
@@ -184,12 +245,7 @@
         keep[slot] = window_mask(doc_ref, start).astype(F32)
         spread[slot] = spread_mask(doc_ref, start, follow).astype(F32).astype(BF16)
         rows = slice(slot * SPAN, (slot + 1) * SPAN)
-        win[slot, :SPAN] = prev_ref[slot]
-        win[slot, SPAN:] = (qkv_ref[1, rows].astype(F32) * qkv_ref[2, rows].astype(F32)).astype(
-            BF16
-        )
         dwin[slot, :SPAN] = dc_ref[rows]
-        dwin[slot, SPAN:] = dcn_ref[slot]
     owner = lax.broadcasted_iota(jnp.int32, (SPAN, LANES), 1) // 16
     tiles = dc_ref.shape[1] // LANES
 
@@ -206,8 +262,6 @@
         out_ref[1, rows, cols] = (total * qkv_ref[2, rows, cols].astype(F32)).astype(BF16)
         out_ref[2, rows, cols] = (total * qkv_ref[1, rows, cols].astype(F32)).astype(BF16)
         return carry
-
-    lax.fori_loop(0, 2 * tiles, tile, 0)
 
     def taps(t, carry):
         cols = pl.ds(pl.multiple_of(t * LANES, LANES), LANES)
@@ -241,13 +295,12 @@
         total = row if r == 0 else total + pltpu.roll(row, 2 * SPAN - r, 1)
     total = pltpu.roll(total, 2 * SPAN - 1, 1)[:, :LANES]
 
-    copies = []
-    for n, buffer in enumerate((tap_y, tap_z, tap_x)):
-        buffer[0] = total
-        sent = [
+    buffers = (tap_y, tap_z, tap_x)
+    taken = [
+        [
             pltpu.make_async_remote_copy(
-                src_ref=buffer.at[0],
-                dst_ref=buffer.at[i + 1],
+                src_ref=buffers[n].at[0],
+                dst_ref=buffers[n].at[i + 1],
                 send_sem=tap_send.at[n, i],
                 recv_sem=tap_recv.at[n, i],
                 device_id=(target, tp),
@@ -255,21 +308,39 @@
             )
             for i, target in enumerate(partners[n])
         ]
-        for copy in sent:
+        for n in range(3)
+    ]
+
+    def give(n, value):
+        buffers[n][0] = value
+        for copy in taken[n]:
             copy.start()
-        for copy in sent:
+
+    def take(n):
+        for copy in taken[n]:
             copy.wait_recv()
-        if n < 2:
-            total = (buffer[0] + buffer[2]) + (buffer[1] + buffer[3])
-        else:
-            total = buffer[0] + buffer[1]
-        copies += sent
-    gf_ref[...] = total
-    for copy in copies:
+        if n == 2:
+            return tap_x[0] + tap_x[1]
+        return (buffers[n][0] + buffers[n][2]) + (buffers[n][1] + buffers[n][3])
+
+    give(0, total)
+    filt = filt_ref[...].astype(F32)
+    sheared(jnp.concatenate([filt, jnp.zeros_like(filt)], axis=1), base)
+    toeplitz(base, toep)
+    give(1, take(0))
+    for slot in range(2):
+        halo[slot].wait_recv()
+    dwin[0, SPAN:] = jnp.where(rank == count - 1, dc_ref[SPAN:], edge[0])
+    dwin[1, SPAN:] = jnp.where(rank == 0, jnp.zeros_like(edge[1]), edge[1])
+    lax.fori_loop(0, tiles, tile, 0)
+    give(2, take(1))
+    lax.fori_loop(tiles, 2 * tiles, tile, 0)
+    gf_ref[...] = take(2)
+    for copy in halo + sum(taken, []):
         copy.wait_send()
 
 
-def back_call(doc_lens, filters, qkv, prev, dc, dcn, gq, count):
+def back_call(doc_lens, filters, qkv, win, dc, gq, count):
     groups = filters.shape[0]
     width = qkv.shape[2]
     return pl.pallas_call(
@@ -279,7 +350,7 @@
             jax.ShapeDtypeStruct((groups, LANES), F32),
         ),
         in_specs=[pl.BlockSpec(memory_space=pltpu.SMEM)]
-        + [pl.BlockSpec(memory_space=pltpu.VMEM)] * 6,
+        + [pl.BlockSpec(memory_space=pltpu.VMEM)] * 5,
         out_specs=(pl.BlockSpec(memory_space=pltpu.VMEM),) * 2,
         scratch_shapes=[
             pltpu.VMEM((2, 8 * groups, SPAN), F32),
@@ -287,19 +358,21 @@
             pltpu.VMEM((2, SPAN, 2 * SPAN), BF16),
             pltpu.VMEM((2, SPAN, 2 * SPAN), F32),
             pltpu.VMEM((2, 2 * SPAN, width), BF16),
-            pltpu.VMEM((2, 2 * SPAN, width), BF16),
+            pltpu.VMEM((2, SPAN, width), BF16),
             pltpu.VMEM((2, 8 * groups, SPAN), F32),
             pltpu.VMEM((4, groups, LANES), F32),
             pltpu.VMEM((4, groups, LANES), F32),
             pltpu.VMEM((2, groups, LANES), F32),
             pltpu.SemaphoreType.DMA((3, 3)),
             pltpu.SemaphoreType.DMA((3, 3)),
+            pltpu.SemaphoreType.DMA((2,)),
+            pltpu.SemaphoreType.DMA((2,)),
         ],
         compiler_params=pltpu.CompilerParams(
             vmem_limit_bytes=40 * 1024 * 1024, collective_id=1, has_side_effects=True
         ),
         name="back",
-    )(doc_lens, filters, qkv, prev, dc, dcn, gq)
+    )(doc_lens, filters, qkv, win, dc, gq)
 
 
 def project_kernel(
@@ -584,25 +657,13 @@
     )(cot, yt, w_out, qkv, c)
 
 
-def neighbours(low, high, count):
-    ahead = lax.ppermute(low, "ctx", [(i, i + 1) for i in range(count - 1)])
-    behind = lax.ppermute(high, "ctx", [(i + 1, i) for i in range(count - 1)])
-    return ahead, behind
-
-
 def local(qkv, filters, w_out, cotangent, doc_lens):
     count = lax.axis_size("ctx")
-    last = lax.axis_index("ctx") == count - 1
     tokens = qkv.shape[1] * count
     scale = 1.0 / math.sqrt(tokens)
-    hidden = (qkv[1].astype(F32) * qkv[2].astype(F32)).astype(BF16)
-    before, after = neighbours(hidden[:SPAN], hidden[SPAN:], count)
-    prev = jnp.stack([before, jnp.where(last, hidden[:SPAN], after)])
-    conv, gated = conv_call(doc_lens, filters, qkv, prev, count)
+    conv, gated, win = conv_call(doc_lens, filters, qkv, count)
     grad_w, grad_c, grad_q = project_call(cotangent, gated, w_out, qkv, conv, scale)
-    before, after = neighbours(grad_c[SPAN:], grad_c[:SPAN], count)
-    follow = jnp.stack([jnp.where(last, grad_c[SPAN:], after), before])
-    grad_qkv, taps = back_call(doc_lens, filters, qkv, prev, grad_c, follow, grad_q, count)
+    grad_qkv, taps = back_call(doc_lens, filters, qkv, win, grad_c, grad_q, count)
     return grad_qkv, jnp.flip(taps, axis=1) * scale, grad_w
 
 

time: 182 us -> 136 us (0.75)
  waiting for transfers between devices: 33.2 us -> 0 us
  starting transfers between devices: 19.9 us -> 0 us
  local copies, waits for them, and re-layouts: 5.21 us -> 11.1 us
  Pallas kernels: 117 us -> 122 us
  other arithmetic: 3.17 us -> 0.63 us
    ppermute x4 -> x0, waiting for transfers between devices: 33.2 us -> none  [the longest x2 23.8 us: neighbours(): ahead = lax.ppermute(low, 'ctx', [(i, i + 1) for i in range(count - 1)])]
    ppermute x4 -> x0, starting transfers between devices: 19.9 us -> none  [the longest x2 16.1 us: neighbours(): behind = lax.ppermute(high, 'ctx', [(i + 1, i) for i in range(count - 1)])]
    unnamed x20 -> x28, local copies, waits for them, and re-layouts: 3.98 us -> 11 us
    pallas_call x1, Pallas kernels: 13.6 us -> 20.4 us  [conv_call(): pl.pallas_call(functools.partial(conv_kernel, count), out_shape=(jax.Shap...]
    pallas_call x1, Pallas kernels: 31.4 us -> 27.1 us  [back_call(): pl.pallas_call(functools.partial(back_kernel, count), out_shape=(jax.Shap...]
    pallas_call x1, Pallas kernels: 71.5 us -> 74.1 us  [project_call(): pl.pallas_call(functools.partial(project_kernel, scale), out_shape=(jax.S...]
  transfers between devices with their start and end apart: 4 -> 0, of which waited for: 4 -> 0; matrix products, arithmetic and copies ran while one was open for 0% -> 0% of each run, Pallas kernels for 0% -> 0%
where the time goes in v3:
time: 136 us; the launch traced here: 134 us
  Pallas kernels  122 us (90%)
  local copies, waits for them, and re-layouts  11.1 us (8%)
    pallas_call x1, Pallas kernels, project_call(): pl.pallas_call(functools.partial(project_kernel, scale), out_shape=(jax.S...  74.1 us
    pallas_call x1, Pallas kernels, back_call(): pl.pallas_call(functools.partial(back_kernel, count), out_shape=(jax.Shap...  27.1 us
    pallas_call x1, Pallas kernels, conv_call(): pl.pallas_call(functools.partial(conv_kernel, count), out_shape=(jax.Shap...  20.4 us
    unnamed x28, local copies, waits for them, and re-layouts  11 us

profile of v3, /device:TPU:4, one launch (start us, length us, event | category | flops | bytes accessed | tf_op | source)
XLA Modules:
  0.0 134.1 jit_solution(9167093459632445598)
XLA Ops:
  0.6 0.0 copy-start
  0.6 1.4 %copy-done = bf16[3,256,1024]{2,1,0:T(8,128)(2,1)S(1)} copy-done((bf16[3,256,1024]{2,1,0:T(8,128)(2,1)S(1)}, bf16[3,256,1024]{2,1,0:T(8,128)(2,1)}, u32[]{:S(2)}) %copy-start) | copy-done | bytes 1572888
  2.0 0.0 copy-start.8
  2.0 0.7 copy-done.8
  2.8 0.0 copy-start.10
  2.8 0.7 copy-done.10
  3.4 20.4 %conv.1 = (f32[256,1024]{1,0:T(8,128)S(1)}, bf16[1024,256]{1,0:T(8,128)(2,1)S(1)}, bf16[2,256,1024]{2,1,0:T(8,128)(2,1)S(1)}) custom-call(s32[64]{0:T(128)S(1)} %copy-done.10, bf16[64,128]{1,0:T(8,128)(2,1)S(1)} %copy-done.8, bf16[3,256,1024]{2,1,0:T(8,128)(2,1)S(1)} %copy-done), custom_call_target="tpu_custom_call" | custom-call | tf_op jit(solution)/shard_map/conv/pallas_call | solution.py:164
  23.8 0.0 copy-start.2
  23.8 1.0 copy-done.2
  24.8 0.0 copy-start.3
  24.8 1.0 copy-done.3
  25.7 0.0 copy-start.5
  25.7 0.8 copy-done.5
  26.5 0.0 copy-start.1
  26.5 0.0 copy-start.9
  26.5 0.0 copy-start.11
  26.5 74.1 %project.1 = (f32[128,1024]{1,0:T(8,128)}, bf16[256,1024]{1,0:T(8,128)(2,1)}, bf16[256,1024]{1,0:T(8,128)(2,1)}) custom-call(bf16[64,4096]{1,0:T(8,128)(2,1)} %cot_ref.1, bf16[1024,256]{1,0:T(8,128)(2,1)} %copy-done.5, bf16[4096,1024]{1,0:T(8,128)(2,1)} %w_ref.1, bf16[3,256,1024]{2,1,0:T(8,128)(2,1)} %qkv_ref.5, f32[256,1024]{1,0:T(8,128)} %copy-done.2), custom_call_target="tpu_custom_call" | custom-call | tf_op jit(solution)/shard_map/project/pallas_call | solution.py:621
  100.7 0.0 copy-done.1
  100.7 0.0 copy-done.9
  100.7 0.0 copy-done.11
  100.7 0.0 copy-start.4
  100.7 1.2 copy-done.4
  102.0 0.0 copy-start.6
  102.0 1.0 copy-done.6
  103.0 0.0 copy-start.7
  103.0 1.0 copy-done.7
  104.0 27.1 %back.1 = (bf16[3,256,1024]{2,1,0:T(8,128)(2,1)S(1)}, f32[64,128]{1,0:T(8,128)S(1)}) custom-call(s32[64]{0:T(128)S(1)} %copy-done.11, bf16[64,128]{1,0:T(8,128)(2,1)S(1)} %copy-done.9, bf16[3,256,1024]{2,1,0:T(8,128)(2,1)S(1)} %copy-done.1, bf16[2,256,1024]{2,1,0:T(8,128)(2,1)S(1)} %copy-done.4, bf16[256,1024]{1,0:T(8,128)(2,1)S(1)} %copy-done.6, ...), custom_call_target="tpu_custom_call" | custom-call | tf_op jit(solution)/shard_map/back/pallas_call | solution.py:346
  131.2 0.1 rev.4
  131.3 0.6 broadcast_multiply_fusion
  131.9 1.1 copy.10
  133.0 0.3 copy-done.12
  133.3 0.8 copy.11
  (1 shorter events, 0.0 us)
Async XLA Ops:
  0.6 1.4 %copy-start = (bf16[3,256,1024]{2,1,0:T(8,128)(2,1)S(1)}, bf16[3,256,1024]{2,1,0:T(8,128)(2,1)}, u32[]{:S(2)}) copy-start(bf16[3,256,1024]{2,1,0:T(8,128)(2,1)} %qkv_ref.5) | copy-start | bytes 4718596
  2.0 0.7 copy-start.8
  2.8 0.7 copy-start.10
  23.8 1.0 copy-start.2
  24.8 1.0 copy-start.3
  25.7 0.8 copy-start.5
  26.5 74.2 %copy-start.1 = (bf16[3,256,1024]{2,1,0:T(8,128)(2,1)S(1)}, bf16[3,256,1024]{2,1,0:T(8,128)(2,1)}, u32[]{:S(2)}) copy-start(bf16[3,256,1024]{2,1,0:T(8,128)(2,1)} %qkv_ref.5) | copy-start | bytes 4718596
  26.5 74.2 %copy-start.9 = (bf16[64,128]{1,0:T(8,128)(2,1)S(1)}, bf16[64,128]{1,0:T(8,128)(2,1)}, u32[]{:S(2)}) copy-start(bf16[64,128]{1,0:T(8,128)(2,1)} %filt_ref.3) | copy-start | bytes 49156
  26.5 74.2 %copy-start.11 = (s32[64]{0:T(128)S(1)}, s32[64]{0:T(128)}, u32[]{:S(2)}) copy-start(s32[64]{0:T(128)} %doc_ref.3) | copy-start | bytes 772
  100.7 1.2 copy-start.4
  102.0 1.0 copy-start.6
  103.0 1.0 copy-start.7
  131.9 1.4 %copy-start.12 = (f32[128,1024]{1,0:T(8,128)S(1)}, f32[128,1024]{1,0:T(8,128)}, u32[]{:S(2)}) copy-start(f32[128,1024]{1,0:T(8,128)} %get-tuple-element.24) | copy-start | bytes 1572868

commit v4 on v3

--- a/solution.py
+++ b/solution.py
@@ -98,28 +98,57 @@
     doc_ref,
     filt_ref,
     qkv_ref,
+    cot_ref,
     c_ref,
     yt_ref,
     win,
+    full_ref,
     base,
     toep,
     mask,
     own,
     edge,
+    full,
     edge_send,
     edge_recv,
+    cot_send,
+    cot_recv,
 ):
     rank = lax.axis_index("ctx")
+    tp = lax.axis_index("tp")
+    core = tp + 1 - 2 * (tp % 2)
+    beside = tp + 2 - 4 * (tp // 2)
+    rows_local = cot_ref.shape[0]
     ends = ((rank + 1) % count, (rank + count - 1) % count)
     barrier = pltpu.get_barrier_semaphore()
     for target in ends:
         pl.semaphore_signal(
-            barrier, inc=1, device_id=(target, lax.axis_index("tp")), device_id_type=MESH
+            barrier, inc=1, device_id=(target, tp), device_id_type=MESH
         )
+    for target in (core, beside):
+        pl.semaphore_signal(barrier, inc=1, device_id=(rank, target), device_id_type=MESH)
     for slot in range(2):
         rows = slice(slot * SPAN, (slot + 1) * SPAN)
         own[slot] = (qkv_ref[1, rows].astype(F32) * qkv_ref[2, rows].astype(F32)).astype(BF16)
-    pl.semaphore_wait(barrier, 2)
+    pl.semaphore_wait(barrier, 4)
+
+    def cot_copy(n, own_rows, source, target):
+        rows = pl.ds(pl.multiple_of(source * rows_local, rows_local), rows_local)
+        return pltpu.make_async_remote_copy(
+            src_ref=cot_ref if own_rows else full.at[rows],
+            dst_ref=full.at[rows],
+            send_sem=cot_send.at[n],
+            recv_sem=cot_recv.at[n],
+            device_id=(rank, target),
+            device_id_type=MESH,
+        )
+
+    side = cot_copy(0, True, tp, beside)
+    near = cot_copy(1, True, tp, core)
+    pass_on = cot_copy(2, False, beside, core)
+    side.start()
+    near.start()
+    full[pl.ds(pl.multiple_of(tp * rows_local, rows_local), rows_local), :] = cot_ref[...]
     halo = halo_copies([own.at[0], own.at[1]], edge, ends, edge_send, edge_recv)
     for copy in halo:
         copy.start()
@@ -153,12 +182,18 @@
         yt_ref[cols, rows] = gated.T.astype(BF16)
         return carry
 
-    lax.fori_loop(0, 2 * tiles, tile, 0)
-    for copy in halo:
+    lax.fori_loop(0, tiles, tile, 0)
+    side.wait_recv()
+    pass_on.start()
+    lax.fori_loop(tiles, 2 * tiles, tile, 0)
+    near.wait_recv()
+    pass_on.wait_recv()
+    full_ref[...] = full[...]
+    for copy in halo + [side, near, pass_on]:
         copy.wait_send()
 
 
-def conv_call(doc_lens, filters, qkv, count):
+def conv_call(doc_lens, filters, qkv, cot, count):
     groups = filters.shape[0]
     width = qkv.shape[2]
     return pl.pallas_call(
@@ -167,24 +202,28 @@
             jax.ShapeDtypeStruct((2 * SPAN, width), F32),
             jax.ShapeDtypeStruct((width, 2 * SPAN), BF16),
             jax.ShapeDtypeStruct((2, 2 * SPAN, width), BF16),
+            jax.ShapeDtypeStruct((2 * SPAN, cot.shape[1]), BF16),
         ),
         in_specs=[pl.BlockSpec(memory_space=pltpu.SMEM)]
-        + [pl.BlockSpec(memory_space=pltpu.VMEM)] * 2,
-        out_specs=(pl.BlockSpec(memory_space=pltpu.VMEM),) * 3,
+        + [pl.BlockSpec(memory_space=pltpu.VMEM)] * 3,
+        out_specs=(pl.BlockSpec(memory_space=pltpu.VMEM),) * 4,
         scratch_shapes=[
             pltpu.VMEM((2, 8 * groups, SPAN), F32),
             pltpu.VMEM((groups, SPAN, 2 * SPAN), BF16),
             pltpu.VMEM((2, SPAN, 2 * SPAN), BF16),
             pltpu.VMEM((2, SPAN, width), BF16),
             pltpu.VMEM((2, SPAN, width), BF16),
+            pltpu.VMEM((2 * SPAN, cot.shape[1]), BF16),
             pltpu.SemaphoreType.DMA((2,)),
             pltpu.SemaphoreType.DMA((2,)),
+            pltpu.SemaphoreType.DMA((3,)),
+            pltpu.SemaphoreType.DMA((3,)),
         ],
         compiler_params=pltpu.CompilerParams(
             vmem_limit_bytes=40 * 1024 * 1024, collective_id=2, has_side_effects=True
         ),
         name="conv",
-    )(doc_lens, filters, qkv)
+    )(doc_lens, filters, qkv, cot)
 
 
 def back_kernel(
@@ -377,7 +416,7 @@
 
 def project_kernel(
     scale,
-    cot_ref,
+    full,
     yt_ref,
     w_ref,
     qkv_ref,
@@ -385,7 +424,6 @@
     gw_ref,
     dc_ref,
     gq_ref,
-    full,
     w_v,
     q_v,
     part,
@@ -398,8 +436,6 @@
     kept,
     far,
     load_sem,
-    cot_send,
-    cot_recv,
     send1,
     recv1,
     send2,
@@ -414,14 +450,11 @@
     my_x = ctx // 16
     place = (my_y, my_z)
     stride = (1, 4)
-    rows_local = cot_ref.shape[0]
 
     def around(axis, step):
         return ctx + stride[axis] * ((place[axis] + step) % 4 - place[axis])
 
     across = ctx + 16 - 32 * my_x
-    core = tp + 1 - 2 * (tp % 2)
-    beside = tp + 2 - 4 * (tp // 2)
 
     barrier = pltpu.get_barrier_semaphore()
     for axis in range(2):
@@ -430,45 +463,18 @@
                 barrier, inc=1, device_id=(around(axis, step), tp), device_id_type=MESH
             )
     pl.semaphore_signal(barrier, inc=1, device_id=(across, tp), device_id_type=MESH)
-    pl.semaphore_signal(barrier, inc=1, device_id=(ctx, core), device_id_type=MESH)
-    pl.semaphore_signal(barrier, inc=1, device_id=(ctx, beside), device_id_type=MESH)
     load_w = pltpu.make_async_copy(w_ref, w_v, load_sem.at[0])
     load_q = pltpu.make_async_copy(qkv_ref.at[0], q_v, load_sem.at[1])
-    pl.semaphore_wait(barrier, 7)
-
-    half_cols = cot_ref.shape[1] // 2
+    pl.semaphore_wait(barrier, 5)
+
+    half_cols = full.shape[1] // 2
     col0 = [
         pl.multiple_of((1 - my_x) * half_cols, half_cols),
         pl.multiple_of(my_x * half_cols, half_cols),
     ]
 
-    def cot_copy(k, n, src, owner, target):
-        rows = pl.ds(pl.multiple_of(owner * rows_local, rows_local), rows_local)
-        cols = pl.ds(col0[k], half_cols)
-        return pltpu.make_async_remote_copy(
-            src_ref=cot_ref.at[:, cols] if src is None else full.at[rows, cols],
-            dst_ref=full.at[rows, cols],
-            send_sem=cot_send.at[k, n],
-            recv_sem=cot_recv.at[k, n],
-            device_id=(ctx, target),
-            device_id_type=MESH,
-        )
-
-    side = [cot_copy(k, 0, None, tp, beside) for k in range(2)]
-    near = [cot_copy(k, 1, None, tp, core) for k in range(2)]
-    pass_on = [cot_copy(k, 2, full, beside, core) for k in range(2)]
-    for k in range(2):
-        side[k].start()
-        near[k].start()
     load_w.start()
     load_q.start()
-    full[pl.ds(pl.multiple_of(tp * rows_local, rows_local), rows_local), :] = cot_ref[...]
-
-    def gather(k):
-        side[k].wait_recv()
-        pass_on[k].start()
-        near[k].wait_recv()
-        pass_on[k].wait_recv()
 
     def partial(k):
         def block(i, carry):
@@ -550,7 +556,6 @@
     second = [[ring(2, axis, k) for axis in range(2)] for k in range(2)]
 
     for k in range(2):
-        gather(k)
         partial(k)
         for axis in range(2):
             first[k][axis][0]()
@@ -604,16 +609,13 @@
         gw_ref[:, rows] = ((kept[rows] + far[rows].astype(F32)) * scale).T
     over.wait_send()
     for k in range(2):
-        side[k].wait_send()
-        near[k].wait_send()
-        pass_on[k].wait_send()
         for axis in range(2):
             for copy in first[k][axis][3] + second[k][axis][3]:
                 copy.wait_send()
 
 
-def project_call(cot, yt, w_out, qkv, c, scale):
-    rows_local, feats = cot.shape
+def project_call(full, yt, w_out, qkv, c, scale):
+    feats = full.shape[1]
     width = w_out.shape[1]
     tokens = qkv.shape[1]
     vm = pl.BlockSpec(memory_space=pltpu.VMEM)
@@ -628,7 +630,6 @@
         in_specs=[vm, vm, hb, hb, vm],
         out_specs=(vm, vm, vm),
         scratch_shapes=[
-            pltpu.VMEM((tokens, feats), BF16),
             pltpu.VMEM((feats, width), BF16),
             pltpu.VMEM((tokens, width), BF16),
             pltpu.VMEM((2, 4, 4, width, LANES), BF16),
@@ -641,8 +642,6 @@
             pltpu.VMEM((width, LANES), F32),
             pltpu.VMEM((width, LANES), BF16),
             pltpu.SemaphoreType.DMA((2,)),
-            pltpu.SemaphoreType.DMA((2, 3)),
-            pltpu.SemaphoreType.DMA((2, 3)),
             pltpu.SemaphoreType.DMA((2, 2, 6)),
             pltpu.SemaphoreType.DMA((2, 2, 6)),
             pltpu.SemaphoreType.DMA((2, 2, 6)),
@@ -654,15 +653,15 @@
             vmem_limit_bytes=60 * 1024 * 1024, collective_id=0, has_side_effects=True
         ),
         name="project",
-    )(cot, yt, w_out, qkv, c)
+    )(full, yt, w_out, qkv, c)
 
 
 def local(qkv, filters, w_out, cotangent, doc_lens):
     count = lax.axis_size("ctx")
     tokens = qkv.shape[1] * count
     scale = 1.0 / math.sqrt(tokens)
-    conv, gated, win = conv_call(doc_lens, filters, qkv, count)
-    grad_w, grad_c, grad_q = project_call(cotangent, gated, w_out, qkv, conv, scale)
+    conv, gated, win, full = conv_call(doc_lens, filters, qkv, cotangent, count)
+    grad_w, grad_c, grad_q = project_call(full, gated, w_out, qkv, conv, scale)
     grad_qkv, taps = back_call(doc_lens, filters, qkv, win, grad_c, grad_q, count)
     return grad_qkv, jnp.flip(taps, axis=1) * scale, grad_w
 

time: 136 us -> 139 us (1.022)
  local copies, waits for them, and re-layouts: 11.1 us -> 13.4 us
    pallas_call x1, Pallas kernels: 20.4 us -> 32 us  [conv_call(): pl.pallas_call(functools.partial(conv_kernel, count), out_shape=(jax.Shap...]
    pallas_call x1, Pallas kernels: 74.1 us -> 64.7 us  [project_call(): pl.pallas_call(functools.partial(project_kernel, scale), out_shape=(jax.S...]
    unnamed x28 -> x32, local copies, waits for them, and re-layouts: 11 us -> 13.4 us
where the time goes in v4:
time: 139 us; the launch traced here: 137 us
  Pallas kernels  123 us (88%)
  local copies, waits for them, and re-layouts  13.4 us (10%)
    pallas_call x1, Pallas kernels, project_call(): pl.pallas_call(functools.partial(project_kernel, scale), out_shape=(jax.S...  64.7 us
    pallas_call x1, Pallas kernels, conv_call(): pl.pallas_call(functools.partial(conv_kernel, count), out_shape=(jax.Shap...  32 us
    pallas_call x1, Pallas kernels, back_call(): pl.pallas_call(functools.partial(back_kernel, count), out_shape=(jax.Shap...  25.8 us
    unnamed x32, local copies, waits for them, and re-layouts  13.4 us

profile of v4, /device:TPU:4, one launch (start us, length us, event | category | flops | bytes accessed | tf_op | source)
XLA Modules:
  0.0 137.3 jit_solution(3090356887954652916)
XLA Ops:
  0.6 0.0 copy-start
  0.6 1.4 %copy-done = bf16[3,256,1024]{2,1,0:T(8,128)(2,1)S(1)} copy-done((bf16[3,256,1024]{2,1,0:T(8,128)(2,1)S(1)}, bf16[3,256,1024]{2,1,0:T(8,128)(2,1)}, u32[]{:S(2)}) %copy-start) | copy-done | bytes 1572888
  2.0 1.0 copy-done.6
  3.1 0.0 copy-start.10
  3.1 0.7 copy-done.10
  3.8 0.7 copy-done.12
  4.5 32.0 %conv.1 = (f32[256,1024]{1,0:T(8,128)S(1)}, bf16[1024,256]{1,0:T(8,128)(2,1)S(1)}, bf16[2,256,1024]{2,1,0:T(8,128)(2,1)S(1)}, bf16[256,4096]{1,0:T(8,128)(2,1)S(1)}) custom-call(s32[64]{0:T(128)S(1)} %copy-done.12, bf16[64,128]{1,0:T(8,128)(2,1)S(1)} %copy-done.10, bf16[3,256,1024]{2,1,0:T(8,128)(2,1)S(1)} %copy-done, bf16[64,4096]{1,0:T(8,128)(2,1)S(1)} %copy-done.6), custom_call_target="tpu_custom_call" | custom-call | tf_op jit(solution)/shard_map/conv/pallas_call | solution.py:199
  36.4 0.0 copy-start.2
  36.4 1.3 copy-done.2
  37.8 0.0 copy-start.3
  37.8 1.0 copy-done.3
  38.7 0.0 copy-start.5
  38.7 1.0 copy-done.5
  39.7 0.0 copy-start.9
  39.7 0.8 copy-done.9
  40.5 0.0 copy-start.1
  40.5 0.0 copy-start.11
  40.5 64.7 %project.1 = (f32[128,1024]{1,0:T(8,128)}, bf16[256,1024]{1,0:T(8,128)(2,1)}, bf16[256,1024]{1,0:T(8,128)(2,1)}) custom-call(bf16[256,4096]{1,0:T(8,128)(2,1)} %copy-done.2, bf16[1024,256]{1,0:T(8,128)(2,1)} %copy-done.9, bf16[4096,1024]{1,0:T(8,128)(2,1)} %w_ref.1, bf16[3,256,1024]{2,1,0:T(8,128)(2,1)} %qkv_ref.5, f32[256,1024]{1,0:T(8,128)} %copy-done.5), custom_call_target="tpu_custom_call" | custom-call | tf_op jit(solution)/shard_map/project/pallas_call | solution.py:623
  105.2 0.0 copy-done.1
  105.2 0.0 copy-done.11
  105.3 0.0 copy-done.13
  105.3 0.0 copy-start.4
  105.3 1.2 copy-done.4
  106.5 0.0 copy-start.7
  106.5 1.0 copy-done.7
  107.5 1.0 copy-done.8
  108.6 25.8 %back.1 = (bf16[3,256,1024]{2,1,0:T(8,128)(2,1)S(1)}, f32[64,128]{1,0:T(8,128)S(1)}) custom-call(s32[64]{0:T(128)S(1)} %copy-done.13, bf16[64,128]{1,0:T(8,128)(2,1)S(1)} %copy-done.11, bf16[3,256,1024]{2,1,0:T(8,128)(2,1)S(1)} %copy-done.1, bf16[2,256,1024]{2,1,0:T(8,128)(2,1)S(1)} %copy-done.4, bf16[256,1024]{1,0:T(8,128)(2,1)S(1)} %copy-done.7, ...), custom_call_target="tpu_custom_call" | custom-call | tf_op jit(solution)/shard_map/back/pallas_call | solution.py:385
  134.4 0.1 rev.4
  134.5 0.6 broadcast_multiply_fusion
  135.1 1.1 copy.10
  136.3 0.3 copy-done.14
  136.5 0.8 copy.11
  (5 shorter events, 0.0 us)
Async XLA Ops:
  0.6 1.4 %copy-start = (bf16[3,256,1024]{2,1,0:T(8,128)(2,1)S(1)}, bf16[3,256,1024]{2,1,0:T(8,128)(2,1)}, u32[]{:S(2)}) copy-start(bf16[3,256,1024]{2,1,0:T(8,128)(2,1)} %qkv_ref.5) | copy-start | bytes 4718596
  2.0 1.0 copy-start.6
  3.1 0.7 copy-start.10
  3.8 0.7 copy-start.12
  36.4 1.3 copy-start.2
  37.8 1.0 copy-start.3
  38.7 1.0 copy-start.5
  39.7 0.8 copy-start.9
  40.5 64.7 %copy-start.1 = (bf16[3,256,1024]{2,1,0:T(8,128)(2,1)S(1)}, bf16[3,256,1024]{2,1,0:T(8,128)(2,1)}, u32[]{:S(2)}) copy-start(bf16[3,256,1024]{2,1,0:T(8,128)(2,1)} %qkv_ref.5) | copy-start | bytes 4718596
  40.5 64.7 %copy-start.11 = (bf16[64,128]{1,0:T(8,128)(2,1)S(1)}, bf16[64,128]{1,0:T(8,128)(2,1)}, u32[]{:S(2)}) copy-start(bf16[64,128]{1,0:T(8,128)(2,1)} %filt_ref.3) | copy-start | bytes 49156
  40.5 64.8 %copy-start.13 = (s32[64]{0:T(128)S(1)}, s32[64]{0:T(128)}, u32[]{:S(2)}) copy-start(s32[64]{0:T(128)} %doc_ref.3) | copy-start | bytes 772
  105.3 1.2 copy-start.4
  106.5 1.0 copy-start.7
  107.5 1.0 copy-start.8
  135.1 1.4 %copy-start.14 = (f32[128,1024]{1,0:T(8,128)S(1)}, f32[128,1024]{1,0:T(8,128)}, u32[]{:S(2)}) copy-start(f32[128,1024]{1,0:T(8,128)} %get-tuple-element.26) | copy-start | bytes 1572868
